TPU v7x, 512 devices: a whole 4x4x16 slice. The times are simulated.
512 devices in a mesh: row: 32 (over z_hi, x, core), col: 16 (over z_lo, y).
Axes of the slice: x: 4, y: 4, z: 16 (z_hi: 4, z_lo: 4; z = z_hi * 4 + z_lo), core: 2. Of those that a mesh axis runs over, the one named last changes fastest.
Arguments:
- positions: float32 [3, 262144], P(None, ('row', 'col')), may hold values from 0 to 170
- velocities: float32 [3, 262144], P(None, ('row', 'col')), may hold values from -6 to 6
- old_forces: float32 [3, 262144], P(None, ('row', 'col')), may hold values from -40 to 40
- types: int32 [262144], P(('row', 'col')), may hold values from 0 to 17
- sigma_table: float32 [18], replicated, may hold values from 0.8 to 1.2
- epsilon_table: float32 [18], replicated, may hold values from 0.1 to 1
- pairs: int32 [32, 16, 2, 128], P('row', 'col'), may hold values from 0 to 127, as said below
- live: int32 [32, 16], P('row', 'col'), may hold values from 56 to 128
Outputs:
- moved: float32 [3, 262144], P(None, ('row', 'col'))
- new_velocities: float32 [3, 262144], P(None, ('row', 'col'))
- new_forces: float32 [3, 262144], P(None, ('row', 'col'))
Inputs may be any that keep to these rules, and one draw needn't show every extreme that they name: pairs[r, c, 0, p] is below 64 and pairs[r, c, 1, p] below 128; the slots of one cell name distinct ordered block pairs.
All inputs are finite; a program needn't handle non-finite values.
Results may differ from a plain program's by a relative error of at most 0.0003.
Values sent between devices are 32-bit elements; how exact they have to be, the bound alone decides.
A program may use at most 64 MiB of HBM per device.

v0:
```python
import jax
import jax.numpy as jnp
from jax import lax
from jax.sharding import PartitionSpec as P

BLK = 128
BPD = 4


time_step = 0.05
cell_side = 5.3
cutoff_sq = 6.25


def pair_terms(row_block, col_block, same, box_len):
    delta = col_block[:3, None, :] - row_block[:3, :, None]
    delta = delta - box_len * jnp.floor(delta / box_len + 0.5)
    radius_sq = jnp.sum(delta * delta, axis=0)
    sig = 0.5 * (row_block[3][:, None] + col_block[3][None, :])
    depth = row_block[4][:, None] * col_block[4][None, :]
    soft_sq = radius_sq + sig * sig
    cube = (sig * sig / soft_sq) ** 3
    energy = 4.0 * depth * (cube * cube - cube)
    slope = 4.0 * depth * (2.0 * cube - 1.0) * (-3.0 * cube / soft_sq)
    weight = 1.0 - radius_sq / cutoff_sq
    coeff = 2.0 * (slope * weight * weight + energy * (-2.0 * weight / cutoff_sq))
    count = row_block.shape[1]
    upper = (jnp.arange(count)[:, None] < jnp.arange(count)[None, :]).astype(jnp.float32)
    keeper = jnp.where(same, upper, jnp.ones_like(upper))
    coeff = jnp.where(radius_sq < cutoff_sq, coeff, 0.0) * keeper
    on_row = jnp.sum(coeff[None] * delta, axis=2)
    on_col = -jnp.sum(coeff[None] * delta, axis=1)
    return (on_row, on_col)


def attach_params(coords, kind_row, sigma_table, root_depth):
    kinds = jnp.arange(sigma_table.shape[0], dtype=jnp.float32)[:, None]
    onehot = (kind_row[None, :] == kinds).astype(jnp.float32)
    sizes = jnp.dot(sigma_table, onehot, precision=lax.Precision.HIGHEST)
    depths = jnp.dot(root_depth, onehot, precision=lax.Precision.HIGHEST)
    return jnp.concatenate([coords, sizes[None, :], depths[None, :]], axis=0)


def body(positions, velocities, old_forces, types, sigma_table, epsilon_table, pairs, live):
    moved = positions + time_step * velocities + 0.5 * time_step * time_step * old_forces
    owned = positions.shape[1]
    per_dev = owned // BLK
    n_cols = lax.axis_size("col")
    n_rows = lax.axis_size("row")
    box_len = jnp.array([BPD * cell_side, n_rows * cell_side, n_cols * cell_side], jnp.float32)[
        :, None, None
    ]
    root_depth = jnp.sqrt(epsilon_table)
    kind_floats = types.astype(jnp.float32)
    packet = attach_params(moved, kind_floats, sigma_table, root_depth)
    row_group = lax.all_gather(packet, "col", axis=1, tiled=True)
    col_group = lax.all_gather(packet, "row", axis=1, tiled=True)
    row_id = lax.axis_index("row")
    col_id = lax.axis_index("col")
    slots = pairs[0, 0]
    used = live[0, 0]

    def one_pair(totals, slot, flag):
        row_forces, col_forces = totals
        first_local = slots[0, slot]
        second_local = slots[1, slot]
        block_x = row_id * (n_cols * per_dev) + first_local
        block_y = (second_local // per_dev * n_cols + col_id) * per_dev + second_local % per_dev
        row_block = lax.dynamic_slice_in_dim(row_group, first_local * BLK, BLK, 1)
        col_block = lax.dynamic_slice_in_dim(col_group, second_local * BLK, BLK, 1)
        on_row, on_col = pair_terms(row_block, col_block, block_x == block_y, box_len)
        old_row = lax.dynamic_slice_in_dim(row_forces, first_local * BLK, BLK, 1)
        row_forces = lax.dynamic_update_slice_in_dim(
            row_forces, old_row + flag * on_row, first_local * BLK, 1
        )
        old_col = lax.dynamic_slice_in_dim(col_forces, second_local * BLK, BLK, 1)
        col_forces = lax.dynamic_update_slice_in_dim(
            col_forces, old_col + flag * on_col, second_local * BLK, 1
        )
        return (row_forces, col_forces)

    def two_pairs(turn, totals):
        totals = one_pair(totals, 2 * turn, 1.0)
        second_flag = (2 * turn + 1 < used).astype(jnp.float32)
        return one_pair(totals, 2 * turn + 1, second_flag)

    start = (
        jnp.zeros((3, row_group.shape[1]), jnp.float32),
        jnp.zeros((3, col_group.shape[1]), jnp.float32),
    )
    row_forces, col_forces = lax.fori_loop(0, (used + 1) // 2, two_pairs, start)
    row_share = lax.psum_scatter(row_forces, "col", scatter_dimension=1, tiled=True)
    col_share = lax.psum_scatter(col_forces, "row", scatter_dimension=1, tiled=True)
    new_forces = row_share + col_share
    new_velocities = velocities + 0.5 * time_step * (old_forces + new_forces)
    return (moved, new_velocities, new_forces)


def solution(mesh):
    in_specs = (
        P(None, ("row", "col")),
        P(None, ("row", "col")),
        P(None, ("row", "col")),
        P(("row", "col")),
        P(),
        P(),
        P("row", "col", None, None),
        P("row", "col"),
    )
    out_specs = (P(None, ("row", "col")), P(None, ("row", "col")), P(None, ("row", "col")))
    return jax.shard_map(body, mesh=mesh, in_specs=in_specs, out_specs=out_specs, check_vma=False)
```

profile of v0, /device:TPU:6, one launch (start us, length us, event | category | flops | bytes accessed | tf_op | source)
XLA Modules:
  0.0 1246.8 jit_solution(16313603841554073678)
XLA Ops:
  10.3 45.2 %all_gather.7 = f32[5,8192]{1,0:T(8,128)S(1)} all-gather(f32[5,512]{1,0:T(8,128)S(1)} %pad_maximum_fusion), channel_id=1, replica_groups=mesh['row'=32,'col'=16] {'col'}, dimensions={1}, use_global_device_ids=true | all-gather | bytes 174080 | tf_op jit(solution)/shard_map/all_gather | solution.py:56
  55.4 48.8 %all_gather.6 = f32[5,16384]{1,0:T(8,128)S(1)} all-gather(f32[5,512]{1,0:T(8,128)S(1)} %pad_maximum_fusion), channel_id=1, replica_groups=mesh['row'=32,'col'=16] {'row'}, dimensions={1}, use_global_device_ids=true | all-gather | bytes 337920 | tf_op jit(solution)/shard_map/all_gather | solution.py:57
  104.3 601.6 %while.16 = (s32[]{:T(128)}, f32[3,8192]{1,0:T(4,128)S(1)}, f32[3,16384]{1,0:T(4,128)S(1)}, s32[]{:T(128)}, s32[2,128]{1,0:T(2,128)}, /*index=5*/f32[5,16384]{1,...) while((s32[]{:T(128)}, f32[3,8192]{1,0:T(4,128)S(1)}, ...), condition=%wide.region_7.8_spmd.clone, body=%wide.region_0.7_spmd.clone.sunk | while | flops 2688590 | bytes 613489 | solution.py:91
  105.0 1.5 constant_dynamic-slice_fusion.15
  118.3 1.5 constant_dynamic-slice_fusion.15
  131.7 1.5 constant_dynamic-slice_fusion.15
  145.1 1.5 constant_dynamic-slice_fusion.15
  171.8 1.5 constant_dynamic-slice_fusion.15
  225.3 1.5 constant_dynamic-slice_fusion.15
  278.8 1.5 constant_dynamic-slice_fusion.15
  332.2 1.5 constant_dynamic-slice_fusion.15
  372.3 1.5 constant_dynamic-slice_fusion.15
  385.7 1.5 constant_dynamic-slice_fusion.15
  425.8 1.5 constant_dynamic-slice_fusion.15
  479.3 1.5 constant_dynamic-slice_fusion.15
  532.7 1.5 constant_dynamic-slice_fusion.15
  586.2 1.5 constant_dynamic-slice_fusion.15
  626.3 1.5 constant_dynamic-slice_fusion.15
  639.7 1.5 constant_dynamic-slice_fusion.15
  679.8 1.5 constant_dynamic-slice_fusion.15
  705.9 2.7 copy.12
  708.6 5.1 copy.14
  713.7 338.1 %reduce-scatter.7.cloned.1.call-done = f32[512,3]{1,0:T(8,128)} async-done(((f32[8192,3]{1,0:T(8,128)}), f32[512,3]{1,0:T(8,128)}) %reduce-scatter.7.cloned.1.call-update) | async-done | bytes 6160
  1052.9 185.4 %reduce-scatter.9.cloned.1.call-done = f32[512,3]{1,0:T(8,128)} async-done(((f32[16384,3]{1,0:T(8,128)}), f32[512,3]{1,0:T(8,128)}) %reduce-scatter.9.cloned.1.call-update) | async-done | bytes 6160
  (815 shorter events, 147.7 us)
Async XLA Ops:
  7.2 2.2 copy-start
  7.2 1044.7 %reduce-scatter.7.cloned.1.call-start = ((), (), s32[]{:S(2)}) async-start(), calls=%async_computation.2 | async-start | bytes 4456448
  10.3 703.4 %copy-start.1 = (f32[3,512]{1,0:T(4,128)}, f32[3,512]{1,0:T(4,128)S(1)}, u32[]{:S(2)}) copy-start(f32[3,512]{1,0:T(4,128)S(1)} %multiply_add_fusion.1) | copy-start | bytes 18436
  708.5 529.8 %reduce-scatter.9.cloned.1.call-start = ((), (), s32[]{:S(2)}) async-start(), calls=%async_computation.3 | async-start | bytes 8650752
  708.6 530.8 %copy-start.2 = (f32[3,512]{1,0:T(4,128)S(1)}, f32[3,512]{1,0:T(4,128)}, u32[]{:S(2)}) copy-start(f32[3,512]{1,0:T(4,128)} %param.13) | copy-start | bytes 18436
  708.6 530.8 %copy-start.3 = (f32[3,512]{1,0:T(4,128)S(1)}, f32[3,512]{1,0:T(4,128)}, u32[]{:S(2)}) copy-start(f32[3,512]{1,0:T(4,128)} %param.12) | copy-start | bytes 18436
Sparse Core Ops, SparseCore 0:
  708.7 343.1 reduce-scatter.6
  1056.4 181.8 reduce-scatter.8
where the time goes:
time: 1260 us; the launch traced here: 1250 us
  waiting for transfers between devices  524 us (42%)
  loops' own time  434 us (34%)
  other arithmetic  101 us (8%)
  blocking collectives  93.9 us (7%)
  local copies, waits for them, and re-layouts  78.9 us (6%)
  between operations  14.8 us (1%)
    unnamed x4, waiting for transfers between devices  524 us
    another operation x1, loops' own time, body(): row_forces, col_forces = lax.fori_loop(0, (used + 1) // 2, two_pairs, start)  434 us
    dynamic_slice x45, local copies, waits for them, and re-layouts, one_pair(): second_local = slots[1, slot]  66.6 us
    all_gather x1, blocking collectives, body(): col_group = lax.all_gather(packet, 'row', axis=1, tiled=True)  48.8 us
    all_gather x1, blocking collectives, body(): row_group = lax.all_gather(packet, 'col', axis=1, tiled=True)  45.2 us
    reduce_sum x45, other arithmetic, pair_terms(): on_col = -jnp.sum(coeff[None] * delta, axis=1)  45 us
    reduce_sum x45, other arithmetic, pair_terms(): radius_sq = jnp.sum(delta * delta, axis=0)  38.9 us
  transfers between devices with their start and end apart: 2, of which 2 were waited for; matrix products, arithmetic and copies ran while one was open for 0% of the time, Pallas kernels for 0%

commit v1 on v0

v1 whole, which is shorter than its diff:
```python
import math

import jax
import jax.numpy as jnp
from jax import lax
from jax.experimental import pallas as pl
from jax.experimental.pallas import tpu as pltpu
from jax.sharding import PartitionSpec as P

BLK = 128
BPD = 4
NZH, NX, NK = 4, 4, 2
NZL, NY = 4, 4
ROWS, COLS = NZH * NX * NK, NZL * NY
NA, NB = COLS * BPD, ROWS * BPD

time_step = 0.05
cell_side = 5.3
cutoff_sq = 6.25

MESH = pl.DeviceIdType.MESH
VMEM = pltpu.VMEM


class Place:
    def __init__(self):
        r, c = lax.axis_index("row"), lax.axis_index("col")
        self.r, self.c = r, c
        self.zh, self.x, self.k = r // (NX * NK), (r // NK) % NX, r % NK
        self.zl, self.y = c // NY, c % NY
        self.z_from = (self.zh + 3 - 2 * self.k) % NZH
        self.z_to = (self.zh + 1 + 2 * self.k) % NZH
        self.z_far = (self.zh + 2) % NZH
        self.x_mates = [(self.x + s) % NX for s in (2, 1, 3)]
        self.zl_mates = [(self.zl + s) % NZL for s in (2, 1, 3)]
        self.y_mates = [(self.y + s) % NY for s in (2, 1, 3)]

    def row_slot(self, zh, x, k):
        return (zh * NX + x) * NK + k

    def col_slot(self, zl, y):
        return zl * NY + y

    def at_z(self, zh):
        return (self.row_slot(zh, self.x, self.k), self.c)

    def at_x(self, x):
        return (self.row_slot(self.zh, x, self.k), self.c)

    def at_core(self):
        return (self.row_slot(self.zh, self.x, 1 - self.k), self.c)

    def at_zl(self, zl):
        return (self.r, self.col_slot(zl, self.y))

    def at_y(self, y):
        return (self.r, self.col_slot(self.zl, y))

    def partners(self):
        return (
            [self.at_z(self.z_from), self.at_z(self.z_to), self.at_core()]
            + [self.at_x(x) for x in self.x_mates]
            + [self.at_zl(z) for z in self.zl_mates]
            + [self.at_y(y) for y in self.y_mates]
        )


def greet(me):
    barrier = pltpu.get_barrier_semaphore()
    for device in me.partners():
        pl.semaphore_signal(barrier, inc=1, device_id=device, device_id_type=MESH)
    return barrier


def gather_kernel(pos, vel, old, kind, row_group, col_group, mine, send_sem, row_sem, col_sem):
    me = Place()
    barrier = greet(me)
    moved = pos[...] + time_step * vel[...] + 0.5 * time_step * time_step * old[...]
    kinds = kind[...]
    for e in range(BPD):
        mine[4 * e : 4 * e + 3, :] = moved[:, BLK * e : BLK * (e + 1)]
        mine[4 * e + 3 : 4 * e + 4, :] = kinds[e : e + 1, :]
    packet = mine[...]
    row_group[pl.ds(pl.multiple_of(me.c * 16, 16), 16), :] = packet
    col_group[pl.ds(pl.multiple_of(me.r * 16, 16), 16), :] = packet
    pl.semaphore_wait(barrier, len(me.partners()))

    started = []

    def ship(src, group, sems, slot, device):
        copy = pltpu.make_async_remote_copy(
            src_ref=src,
            dst_ref=group.at[pl.ds(pl.multiple_of(slot * 16, 16), 16), :],
            send_sem=send_sem.at[len(started)],
            recv_sem=sems.at[slot],
            device_id=device,
            device_id_type=MESH,
        )
        copy.start()
        started.append(copy)

    def arrived(group, sems, slot):
        view = group.at[pl.ds(pl.multiple_of(slot * 16, 16), 16), :]
        pltpu.make_async_remote_copy(
            src_ref=view,
            dst_ref=view,
            send_sem=send_sem.at[0],
            recv_sem=sems.at[slot],
            device_id=me.at_core(),
            device_id_type=MESH,
        ).wait_recv()
        return view

    own_row = me.row_slot(me.zh, me.x, me.k)
    for zh in (me.z_to, me.z_from):
        ship(mine, col_group, col_sem, own_row, me.at_z(zh))
    for zl in me.zl_mates:
        ship(mine, row_group, row_sem, me.c, me.at_zl(zl))
    for x in me.x_mates:
        ship(mine, col_group, col_sem, own_row, me.at_x(x))
    for y in me.y_mates:
        ship(mine, row_group, row_sem, me.c, me.at_y(y))
    ship(mine, col_group, col_sem, own_row, me.at_core())

    def spread(zh, relay):
        slot = me.row_slot(zh, me.x, me.k)
        view = arrived(col_group, col_sem, slot)
        if relay:
            ship(view, col_group, col_sem, slot, me.at_z(me.z_to))
        for x in me.x_mates:
            ship(view, col_group, col_sem, slot, me.at_x(x))
        ship(view, col_group, col_sem, slot, me.at_core())

    def share(zh, x):
        slot = me.row_slot(zh, x, me.k)
        view = arrived(col_group, col_sem, slot)
        ship(view, col_group, col_sem, slot, me.at_core())

    def fan_out(zl):
        slot = me.col_slot(zl, me.y)
        view = arrived(row_group, row_sem, slot)
        for y in me.y_mates:
            ship(view, row_group, row_sem, slot, me.at_y(y))

    for zl in me.zl_mates[1:]:
        fan_out(zl)
    for x in me.x_mates:
        share(me.zh, x)
    fan_out(me.zl_mates[0])
    spread(me.z_from, True)
    spread(me.z_to, False)
    for x in me.x_mates:
        share(me.z_from, x)
        share(me.z_to, x)
    spread(me.z_far, False)
    for x in me.x_mates:
        share(me.z_far, x)
    for y in me.y_mates:
        for zl in range(NZL):
            arrived(row_group, row_sem, me.col_slot(zl, y))
    for zh in range(NZH):
        for x in range(NX):
            arrived(col_group, col_sem, me.row_slot(zh, x, 1 - me.k))
    for copy in started:
        copy.wait_send()


def pair_kernel(
    box_y, box_z, pairs, live, sigma, epsilon, row_group, col_group, on_row, on_col, rows, cols, row_parts, col_parts
):
    sub = lax.broadcasted_iota(jnp.int32, (8, BLK), 0)
    lane = lax.broadcasted_iota(jnp.int32, (8, BLK), 1)
    sizes = jnp.zeros((8, BLK), jnp.float32)
    wells = jnp.zeros((8, BLK), jnp.float32)
    for n in range(sigma.shape[0]):
        sizes = jnp.where(lane == n, 0.5 * sigma[n], sizes)
        wells = jnp.where(lane == n, epsilon[n], wells)
    wells = math.sqrt(8.0) * jnp.sqrt(wells)
    kind_row = (sub == 3) | (sub == 7)

    def prepare(group, table, parts):
        def two_blocks(g, carry):
            both = group[pl.ds(pl.multiple_of(8 * g, 8), 8), :]
            low = jnp.min(both, axis=1, keepdims=True)
            high = jnp.max(both, axis=1, keepdims=True)
            center = jnp.broadcast_to(0.5 * (low + high), (8, BLK))
            near = both - center
            kinds = jnp.where(kind_row, both, 0.0).astype(jnp.int32)
            size = jnp.take_along_axis(sizes, kinds, axis=1, mode="promise_in_bounds")
            well = jnp.take_along_axis(wells, kinds, axis=1, mode="promise_in_bounds")
            for h in range(2):
                at = 4 * h
                tile = jnp.concatenate(
                    [near[at : at + 3], size[at + 3 : at + 4], well[at + 3 : at + 4], center[at : at + 3]], axis=0
                )
                table[2 * g + h] = tile
                coords = jnp.where(sub < 3, tile, jnp.where(sub == 3, 1.0, 0.0))
                head = coords.astype(jnp.bfloat16)
                tail = coords - head.astype(jnp.float32)
                parts[2 * g + h] = jnp.concatenate([head.astype(jnp.float32), tail], axis=0).astype(jnp.bfloat16)
            return carry

        lax.fori_loop(0, group.shape[0] // 8, two_blocks, 0, unroll=4)

    prepare(row_group, rows, row_parts)
    prepare(col_group, cols, col_parts)
    on_row[...] = jnp.zeros_like(on_row)
    on_col[...] = jnp.zeros_like(on_col)

    row_id, col_id = lax.axis_index("row"), lax.axis_index("col")
    box = jnp.where(sub == 5, BPD * cell_side, jnp.where(sub == 6, box_y, box_z))
    inverse_box = 1.0 / box

    def one_pair(p, carry):
        a, b = pairs[0, p], pairs[1, p]
        mine, theirs = rows[a], cols[b]
        apart = theirs - mine
        apart = apart - box * jnp.floor(apart * inverse_box + 0.5)
        shift = jnp.where(sub < 3, pltpu.roll(apart, 3, 0), 0.0)
        other = theirs + shift
        turned = mine.T
        heads, tails = [], []
        for n in range(0, BLK, 16):
            part = turned[n : n + 16]
            dx = other[0:1] - part[:, 0:1]
            dy = other[1:2] - part[:, 1:2]
            dz = other[2:3] - part[:, 2:3]
            sig = other[3:4] + part[:, 3:4]
            well = other[4:5] * part[:, 4:5]
            r2 = dx * dx + dy * dy + dz * dz
            sig2 = sig * sig
            soft = r2 + sig2
            guess = pl.reciprocal(soft, approx=True)
            inv = guess * (2.0 - soft * guess)
            ratio = sig2 * inv
            u3 = ratio * ratio * ratio
            w = jnp.maximum(1.0 - r2 * (1.0 / cutoff_sq), 0.0)
            lead = (3.0 - 6.0 * u3) * (inv * w)
            rest = (2.0 / cutoff_sq) - (2.0 / cutoff_sq) * u3
            k = (lead + rest) * (u3 * w * well)
            head = k.astype(jnp.bfloat16)
            heads.append(head)
            tails.append((k - head.astype(jnp.float32)).astype(jnp.bfloat16))
        head, tail = jnp.concatenate(heads, axis=0), jnp.concatenate(tails, axis=0)
        px, py = row_parts[a], col_parts[b]
        across = (((1,), (1,)), ((), ()))
        down = (((1,), (0,)), ((), ()))
        vr = lax.dot_general(py, head, across, preferred_element_type=jnp.float32) + lax.dot_general(
            py, tail, across, preferred_element_type=jnp.float32
        )
        vc = lax.dot_general(px, head, down, preferred_element_type=jnp.float32) + lax.dot_general(
            px, tail, down, preferred_element_type=jnp.float32
        )
        vr, vc = vr[0:8] + vr[8:16], vc[0:8] + vc[8:16]
        mine_r = px[0:8].astype(jnp.float32) + px[8:16].astype(jnp.float32)
        theirs_r = py[0:8].astype(jnp.float32) + py[8:16].astype(jnp.float32)
        fr = vr + (shift - mine_r) * vr[3:4]
        fc = vc - (shift + theirs_r) * vc[3:4]
        same = (b // BPD == row_id) & (a == col_id * BPD + b % BPD)
        fc = fc * jnp.where(same, 0.0, 1.0)
        on_row[a] = on_row[a] + fr[0:4]
        on_col[b] = on_col[b] + fc[0:4]
        return carry

    lax.fori_loop(0, live[0], one_pair, 0)


def scatter_kernel(
    on_row, on_col, old, vel, force, new_vel,
    core_in, x_out, x_in, z_out, z_relay, z_in, y_in, zl_out, zl_in,
    send_sem, core_sem, x_sem, z_sem, y_sem, zl_sem,
):
    me = Place()
    barrier = greet(me)
    pl.semaphore_wait(barrier, len(me.partners()))
    started = []

    def ship(src, dst, sem, device):
        copy = pltpu.make_async_remote_copy(
            src_ref=src, dst_ref=dst, send_sem=send_sem.at[len(started)], recv_sem=sem,
            device_id=device, device_id_type=MESH,
        )
        copy.start()
        started.append(copy)

    def arrived(dst, sem):
        pltpu.make_async_remote_copy(
            src_ref=dst, dst_ref=dst, send_sem=send_sem.at[0], recv_sem=sem,
            device_id=me.at_core(), device_id_type=MESH,
        ).wait_recv()

    xs = me.x_mates + [me.x]
    for x in xs:
        ship(on_col.at[:, x, 1 - me.k], core_in.at[x], core_sem.at[x], me.at_core())
    for y in me.y_mates:
        ship(on_row.at[:, y], y_in.at[me.y], y_sem.at[me.y], me.at_y(y))
    for x in me.x_mates:
        arrived(core_in.at[x], core_sem.at[x])
        x_out[x] = on_col[:, x, me.k] + core_in[x]
        ship(x_out.at[x], x_in.at[me.x], x_sem.at[me.x], me.at_x(x))
    arrived(core_in.at[me.x], core_sem.at[me.x])
    own = on_col[:, me.x, me.k] + core_in[me.x]

    total = on_row[:, me.y]
    for y in (me.y_mates[1], me.y_mates[2], me.y_mates[0]):
        arrived(y_in.at[y], y_sem.at[y])
        total = total + y_in[y]
    zl_out[...] = total
    for zl in me.zl_mates:
        ship(zl_out.at[zl], zl_in.at[me.zl], zl_sem.at[me.zl], me.at_zl(zl))

    for x in (me.x_mates[1], me.x_mates[2], me.x_mates[0]):
        arrived(x_in.at[x], x_sem.at[x])
        own = own + x_in[x]
    z_out[...] = own
    ship(z_out.at[me.z_far], z_in.at[0], z_sem.at[0], me.at_z(me.z_to))
    ship(z_out.at[me.z_from], z_in.at[1], z_sem.at[1], me.at_z(me.z_from))

    result = zl_out[me.zl] + z_out[me.zh]
    for zl in me.zl_mates:
        arrived(zl_in.at[zl], zl_sem.at[zl])
        result = result + zl_in[zl]
    arrived(z_in.at[0], z_sem.at[0])
    z_relay[...] = z_in[0] + z_out[me.z_to]
    ship(z_relay, z_in.at[2], z_sem.at[2], me.at_z(me.z_to))
    arrived(z_in.at[1], z_sem.at[1])
    result = result + z_in[1]
    arrived(z_in.at[2], z_sem.at[2])
    result = result + z_in[2]
    for e in range(BPD):
        force[:, BLK * e : BLK * (e + 1)] = result[e, 0:3]
    new_vel[...] = vel[...] + 0.5 * time_step * (old[...] + force[...])
    for copy in started:
        copy.wait_send()


def body(positions, velocities, old_forces, types, sigma_table, epsilon_table, pairs, live):
    f32 = jnp.float32
    dma = pltpu.SemaphoreType.DMA
    moved = positions + time_step * velocities + 0.5 * time_step * time_step * old_forces
    kinds = types.astype(f32).reshape(BPD, BLK)
    vmem = pl.BlockSpec(memory_space=VMEM)
    smem = pl.BlockSpec(memory_space=pltpu.SMEM)
    row_group, col_group = pl.pallas_call(
        gather_kernel,
        out_shape=(
            jax.ShapeDtypeStruct((NA * 4, BLK), f32),
            jax.ShapeDtypeStruct((NB * 4, BLK), f32),
        ),
        in_specs=[vmem] * 4,
        out_specs=(vmem, vmem),
        scratch_shapes=[VMEM((4 * BPD, BLK), f32), dma((48,)), dma((COLS,)), dma((ROWS,))],
        compiler_params=pltpu.CompilerParams(collective_id=0, has_side_effects=True),
        name="gather",
    )(positions, velocities, old_forces, kinds)

    def pair_call(*refs):
        return pair_kernel(ROWS * cell_side, COLS * cell_side, *refs)

    on_row, on_col = pl.pallas_call(
        pair_call,
        out_shape=(
            jax.ShapeDtypeStruct((NA, 4, BLK), f32),
            jax.ShapeDtypeStruct((NB, 4, BLK), f32),
        ),
        in_specs=[smem] * 4 + [vmem] * 2,
        out_specs=(vmem, vmem),
        scratch_shapes=[
            VMEM((NA, 8, BLK), f32),
            VMEM((NB, 8, BLK), f32),
            VMEM((NA, 16, BLK), jnp.bfloat16),
            VMEM((NB, 16, BLK), jnp.bfloat16),
        ],
        name="pairs",
    )(pairs.reshape(2, -1), live.reshape(1), sigma_table, epsilon_table, row_group, col_group)

    tile = (BPD, 4, BLK)
    new_forces, new_velocities = pl.pallas_call(
        scatter_kernel,
        out_shape=(jax.ShapeDtypeStruct(positions.shape, f32), jax.ShapeDtypeStruct(positions.shape, f32)),
        in_specs=[vmem] * 4,
        out_specs=(vmem, vmem),
        scratch_shapes=[
            VMEM((NX, NZH) + tile, f32),
            VMEM((NX, NZH) + tile, f32),
            VMEM((NX, NZH) + tile, f32),
            VMEM((NZH,) + tile, f32),
            VMEM(tile, f32),
            VMEM((3,) + tile, f32),
            VMEM((NY, NZL) + tile, f32),
            VMEM((NZL,) + tile, f32),
            VMEM((NZL,) + tile, f32),
            dma((16,)),
            dma((NX,)),
            dma((NX,)),
            dma((3,)),
            dma((NY,)),
            dma((NZL,)),
        ],
        compiler_params=pltpu.CompilerParams(collective_id=1, has_side_effects=True),
        name="scatter",
    )(
        on_row.reshape((NZL, NY) + tile),
        on_col.reshape((NZH, NX, NK) + tile),
        old_forces,
        velocities,
    )
    return moved, new_velocities, new_forces


def solution(mesh):
    in_specs = (
        P(None, ("row", "col")),
        P(None, ("row", "col")),
        P(None, ("row", "col")),
        P(("row", "col")),
        P(),
        P(),
        P("row", "col", None, None),
        P("row", "col"),
    )
    out_specs = (P(None, ("row", "col")), P(None, ("row", "col")), P(None, ("row", "col")))
    return jax.shard_map(body, mesh=mesh, in_specs=in_specs, out_specs=out_specs, check_vma=False)
```

time: 1260 us -> 115 us (0.09)
  waiting for transfers between devices: 524 us -> 0 us
  loops' own time: 434 us -> 0 us
  Pallas kernels: 0 us -> 108 us
  other arithmetic: 101 us -> 1.87 us
  blocking collectives: 93.9 us -> 0 us
  local copies, waits for them, and re-layouts: 78.9 us -> 1.39 us
  between operations: 14.8 us -> 1.33 us
    unnamed x4 -> x0, waiting for transfers between devices: 524 us -> none
    another operation x1 -> x0, loops' own time: 434 us -> none  [body(): row_forces, col_forces = lax.fori_loop(0, (used + 1) // 2, two_pairs, start)]
    pallas_call x0 -> x3, Pallas kernels: none -> 108 us  [the longest x1 43.8 us: body(): pl.pallas_call(scatter_kernel, out_shape=(jax.ShapeDtypeStruct(positions....]
    all_gather x2 -> x0, blocking collectives: 93.9 us -> none  [the longest x1 48.8 us: body(): col_group = lax.all_gather(packet, 'row', axis=1, tiled=True)]
    reduce_sum x90 -> x0, other arithmetic: 84 us -> none  [the longest x45 45 us: pair_terms(): on_col = -jnp.sum(coeff[None] * delta, axis=1)]
    dynamic_slice x135 -> x0, local copies, waits for them, and re-layouts: 67.6 us -> none  [the longest x45 66.6 us: one_pair(): second_local = slots[1, slot]]
  transfers between devices with their start and end apart: 2 -> 0, of which waited for: 2 -> 0; matrix products, arithmetic and copies ran while one was open for 0% -> 0% of each run, Pallas kernels for 0% -> 0%
where the time goes in v1:
time: 115 us; the launch traced here: 113 us
  Pallas kernels  108 us (94%)
  other arithmetic  1.87 us (2%)
  local copies, waits for them, and re-layouts  1.39 us (1%)
  between operations  1.33 us (1%)
    pallas_call x1, Pallas kernels, body(): pl.pallas_call(scatter_kernel, out_shape=(jax.ShapeDtypeStruct(positions....  43.8 us
    pallas_call x1, Pallas kernels, body(): pl.pallas_call(pair_call, out_shape=(jax.ShapeDtypeStruct((NA, 4, BLK), f...  36.7 us
    pallas_call x1, Pallas kernels, body(): pl.pallas_call(gather_kernel, out_shape=(jax.ShapeDtypeStruct((NA * 4, BL...  27.7 us

profile of v1, /device:TPU:6, one launch (start us, length us, event | category | flops | bytes accessed | tf_op | source)
XLA Modules:
  0.0 112.8 jit_solution(176694062646793937)
XLA Ops:
  0.6 1.3 %convert_bitcast_fusion.kind = f32[4,128]{1,0:T(4,128)} fusion(s32[512]{0:T(512)} %param.11), kind=kLoop, calls=%fused_computation.1 | loop fusion | flops 512 | bytes 4096 | tf_op jit(solution)/shard_map/reshape | solution.py:341
  1.9 27.7 %gather.1 = (f32[256,128]{1,0:T(8,128)}, f32[512,128]{1,0:T(8,128)}) custom-call(f32[3,512]{1,0:T(4,128)} %pos.1, f32[3,512]{1,0:T(4,128)} %vel.3, f32[3,512]{1,0:T(4,128)} %old.3, f32[4,128]{1,0:T(4,128)} %convert_bitcast_fusion.kind), custom_call_target="tpu_custom_call" | custom-call | tf_op jit(solution)/shard_map/gather/pallas_call | solution.py:344
  30.3 36.7 %pairs.1 = (f32[64,4,128]{2,1,0:T(4,128)}, f32[128,4,128]{2,1,0:T(4,128)}) custom-call(s32[2,128]{1,0:T(2,128)} %bitcast.9, s32[1]{0:T(128)} %bitcast.6.refs_1_, f32[18]{0:T(128)} %refs_2_.1, f32[18]{0:T(128)} %refs_3_.1, f32[256,128]{1,0:T(8,128)} %get-tuple-element.9.refs_4_, f32[512,128]{1,0:T(8,128)} %get-tuple-element.10.refs_5_), custom_call_target="tpu_custom_call" | custom-call | tf_op jit(solution)/shard_map/pairs/pallas_call | solution.py:360
  67.0 0.0 copy-start
  67.0 0.0 copy-start.1
  67.0 0.0 copy-start.2
  67.0 43.8 %scatter.1 = (f32[3,512]{1,0:T(4,128)}, f32[3,512]{1,0:T(4,128)}) custom-call(f32[4,4,4,4,128]{4,3,2,1,0:T(4,128)} %bitcast.8, f32[4,4,2,4,4,128]{5,4,3,2,1,0:T(4,128)} %bitcast.7, f32[3,512]{1,0:T(4,128)} %old.3, f32[3,512]{1,0:T(4,128)} %vel.3), custom_call_target="tpu_custom_call" | custom-call | tf_op jit(solution)/shard_map/scatter/pallas_call | solution.py:378
  110.8 0.0 copy-done
  110.8 0.0 copy-done.1
  110.8 0.0 copy-done.2
  110.8 0.0 copy-start.4
  110.9 0.6 multiply_add_fusion
  111.5 0.1 copy-done.4
  111.5 0.0 copy-start.3
  111.5 0.6 copy.14
  112.1 0.1 copy-done.3
  112.2 0.6 copy.15
Async XLA Ops:
  67.0 43.8 %copy-start = (f32[3,512]{1,0:T(4,128)S(1)}, f32[3,512]{1,0:T(4,128)}, u32[]{:S(2)}) copy-start(f32[3,512]{1,0:T(4,128)} %old.3) | copy-start | bytes 18436
  67.0 43.8 %copy-start.1 = (f32[3,512]{1,0:T(4,128)S(1)}, f32[3,512]{1,0:T(4,128)}, u32[]{:S(2)}) copy-start(f32[3,512]{1,0:T(4,128)} %vel.3) | copy-start | bytes 18436
  67.0 43.9 %copy-start.2 = (f32[3,512]{1,0:T(4,128)S(1)}, f32[3,512]{1,0:T(4,128)}, u32[]{:S(2)}) copy-start(f32[3,512]{1,0:T(4,128)} %pos.1) | copy-start | bytes 18436
  110.8 0.7 copy-start.4
  111.5 0.7 copy-start.3

commit v2 on v1

--- a/solution.py
+++ b/solution.py
@@ -76,7 +76,7 @@
     me = Place()
     barrier = greet(me)
     moved = pos[...] + time_step * vel[...] + 0.5 * time_step * time_step * old[...]
-    kinds = kind[...]
+    kinds = kind[...].astype(jnp.float32)
     for e in range(BPD):
         mine[4 * e : 4 * e + 3, :] = moved[:, BLK * e : BLK * (e + 1)]
         mine[4 * e + 3 : 4 * e + 4, :] = kinds[e : e + 1, :]
@@ -165,108 +165,183 @@
         copy.wait_send()
 
 
+def split3(v):
+    head = v.astype(jnp.bfloat16).astype(jnp.float32)
+    rest = v - head
+    mid = rest.astype(jnp.bfloat16).astype(jnp.float32)
+    return head, mid, rest - mid
+
+
 def pair_kernel(
-    box_y, box_z, pairs, live, sigma, epsilon, row_group, col_group, on_row, on_col, rows, cols, row_parts, col_parts
+    box_y, box_z, pairs, live, sigma, epsilon, row_group, col_group, pos, vel, old, on_row, on_col, moved,
+    rows, cols, row_mid, col_mid, row_acc, col_acc, listed, todo, terms, k_head, k_tail, sem,
 ):
+    f32, bf16 = jnp.float32, jnp.bfloat16
+    moved[...] = pos[...] + time_step * vel[...] + 0.5 * time_step * time_step * old[...]
     sub = lax.broadcasted_iota(jnp.int32, (8, BLK), 0)
     lane = lax.broadcasted_iota(jnp.int32, (8, BLK), 1)
-    sizes = jnp.zeros((8, BLK), jnp.float32)
-    wells = jnp.zeros((8, BLK), jnp.float32)
+    sizes = jnp.zeros((8, BLK), f32)
+    wells = jnp.zeros((8, BLK), f32)
     for n in range(sigma.shape[0]):
         sizes = jnp.where(lane == n, 0.5 * sigma[n], sizes)
         wells = jnp.where(lane == n, epsilon[n], wells)
-    wells = math.sqrt(8.0) * jnp.sqrt(wells)
+    wells = math.sqrt(16.0 / cutoff_sq) * jnp.sqrt(wells)
     kind_row = (sub == 3) | (sub == 7)
-
-    def prepare(group, table, parts):
-        def two_blocks(g, carry):
+    box = jnp.where(sub == 0, BPD * cell_side, jnp.where(sub == 1, box_y, jnp.where(sub == 2, box_z, 1.0)))
+    inverse_box = 1.0 / box
+
+    def wrap(v):
+        return v - box * jnp.floor(v * inverse_box + 0.5)
+
+    def prepare(group, table, middle):
+        def two_blocks(g, bounds):
             both = group[pl.ds(pl.multiple_of(8 * g, 8), 8), :]
-            low = jnp.min(both, axis=1, keepdims=True)
-            high = jnp.max(both, axis=1, keepdims=True)
-            center = jnp.broadcast_to(0.5 * (low + high), (8, BLK))
+            low = jnp.broadcast_to(jnp.min(both, axis=1, keepdims=True), (8, BLK))
+            high = jnp.broadcast_to(jnp.max(both, axis=1, keepdims=True), (8, BLK))
+            center = 0.5 * (low + high)
             near = both - center
             kinds = jnp.where(kind_row, both, 0.0).astype(jnp.int32)
             size = jnp.take_along_axis(sizes, kinds, axis=1, mode="promise_in_bounds")
-            well = jnp.take_along_axis(wells, kinds, axis=1, mode="promise_in_bounds")
+            well = pltpu.roll(jnp.take_along_axis(wells, kinds, axis=1, mode="promise_in_bounds"), 1, 0)
+            mixed = jnp.where(kind_row, size, near)
             for h in range(2):
-                at = 4 * h
-                tile = jnp.concatenate(
-                    [near[at : at + 3], size[at + 3 : at + 4], well[at + 3 : at + 4], center[at : at + 3]], axis=0
-                )
-                table[2 * g + h] = tile
-                coords = jnp.where(sub < 3, tile, jnp.where(sub == 3, 1.0, 0.0))
-                head = coords.astype(jnp.bfloat16)
-                tail = coords - head.astype(jnp.float32)
-                parts[2 * g + h] = jnp.concatenate([head.astype(jnp.float32), tail], axis=0).astype(jnp.bfloat16)
-            return carry
-
-        lax.fori_loop(0, group.shape[0] // 8, two_blocks, 0, unroll=4)
-
-    prepare(row_group, rows, row_parts)
-    prepare(col_group, cols, col_parts)
-    on_row[...] = jnp.zeros_like(on_row)
-    on_col[...] = jnp.zeros_like(on_col)
-
+                part = mixed if h == 0 else pltpu.roll(mixed, 4, 0)
+                deep = well if h == 0 else pltpu.roll(well, 4, 0)
+                mid = center if h == 0 else pltpu.roll(center, 4, 0)
+                table[2 * g + h] = jnp.where(sub < 4, part, jnp.where(sub == 4, deep, 0.0))
+                middle[2 * g + h] = jnp.where(sub < 3, mid, 0.0)
+            here = lane == g
+            return jnp.where(here, low, bounds[0]), jnp.where(here, high, bounds[1])
+
+        start = group[0:8, :]
+        return lax.fori_loop(0, group.shape[0] // 8, two_blocks, (start, start), unroll=4)
+
+    row_low, row_high = prepare(row_group, rows, row_mid)
+    col_low, col_high = prepare(col_group, cols, col_mid)
+
+    firsts = jnp.broadcast_to(pairs[0:1, :], (8, BLK))
+    seconds = jnp.broadcast_to(pairs[1:2, :], (8, BLK))
+
+    def pick(bound, index):
+        got = jnp.take_along_axis(bound, index >> 1, axis=1, mode="promise_in_bounds")
+        return jnp.where((index & 1) == 1, pltpu.roll(got, 4, 0), got)
+
+    xl, xh = pick(row_low, firsts), pick(row_high, firsts)
+    yl, yh = pick(col_low, seconds), pick(col_high, seconds)
+    apart = wrap(jnp.where(sub < 3, 0.5 * ((yl + yh) - (xl + xh)), 0.0))
+    gap = jnp.abs(apart) - 0.5 * ((yh - yl) + (xh - xl))
+    gap = jnp.where(sub < 3, jnp.maximum(gap, 0.0), 0.0)
+    gap2 = jnp.sum(gap * gap, axis=0, keepdims=True)
+    near_by = jnp.broadcast_to(gap2, (8, BLK)) < cutoff_sq + 0.01
+    active = jnp.where(near_by & (lane < live[0, 0]), 1.0, 0.0)
+    big_sub = lax.broadcasted_iota(jnp.int32, (BLK, BLK), 0)
+    big_lane = lax.broadcasted_iota(jnp.int32, (BLK, BLK), 1)
+    across = (((1,), (1,)), ((), ()))
+    down = (((1,), (0,)), ((), ()))
+
+    def dot(u, v, dims):
+        return lax.dot_general(u, v, dims, preferred_element_type=f32)
+
+    upto = dot(jnp.where(big_lane <= big_sub, 1.0, 0.0).astype(bf16), active.astype(bf16), across)[:, 0:1]
+    before = dot(jnp.where(big_lane < big_sub, 1.0, 0.0).astype(bf16), active.astype(bf16), across)[:, 0:1]
+    place = big_lane.astype(f32)
+    move = jnp.where((place >= before) & (place < upto), 1.0, 0.0).astype(bf16)
+    both = jnp.where(sub == 0, firsts, seconds).astype(f32).astype(bf16)
+    packed = dot(both, move, down)
+    count = jnp.broadcast_to(jnp.sum(active, axis=1, keepdims=True), (8, BLK))
+    spare = jnp.where(sub == 0, float(NA), float(NB))
+    packed = jnp.where(lane.astype(f32) < count, packed, spare)
+    listed[...] = jnp.where(sub == 2, count, packed).astype(jnp.int32)
+    copy = pltpu.make_async_copy(listed, todo, sem)
+    copy.start()
+    row_acc[...] = jnp.zeros_like(row_acc)
+    col_acc[...] = jnp.zeros_like(col_acc)
+    copy.wait()
+    total = todo[2, 0]
     row_id, col_id = lax.axis_index("row"), lax.axis_index("col")
-    box = jnp.where(sub == 5, BPD * cell_side, jnp.where(sub == 6, box_y, box_z))
-    inverse_box = 1.0 / box
-
-    def one_pair(p, carry):
-        a, b = pairs[0, p], pairs[1, p]
-        mine, theirs = rows[a], cols[b]
-        apart = theirs - mine
-        apart = apart - box * jnp.floor(apart * inverse_box + 0.5)
-        shift = jnp.where(sub < 3, pltpu.roll(apart, 3, 0), 0.0)
-        other = theirs + shift
-        turned = mine.T
-        heads, tails = [], []
+    scale = 1.5 * cutoff_sq
+
+    def force_sources(tile):
+        well = tile[4:5]
+        v = jnp.where(sub < 3, tile * well, jnp.where(sub == 3, well, 0.0))
+        head, mid, low = split3(v)
+        first = jnp.where(sub < 4, head, pltpu.roll(low, 4, 0))
+        return jnp.concatenate([first, mid], axis=0).astype(bf16)
+
+    def fold(v):
+        v = v[0:8] + v[8:16]
+        return v + pltpu.roll(v, 4, 0)
+
+    def turn(p, carry):
+        a1, b1, a2, b2, shift1, shift2 = carry
+        mine, theirs = rows[a2], cols[b2]
+        px, py = force_sources(mine), force_sources(theirs)
+        head, tail = k_head[...], k_tail[...]
+        vr = fold(dot(py, head, across) + dot(py, tail, across))
+        vc = fold(dot(px, head, down) + dot(px, tail, down))
+        fr = (vr + (shift2 - mine) * vr[3:4]) * mine[4:5]
+        fc = (vc - (shift2 + theirs) * vc[3:4]) * theirs[4:5]
+        same = (b2 // BPD == row_id) & (a2 == col_id * BPD + b2 % BPD)
+        fc = fc * jnp.where(same, 0.0, 1.0)
+        row_acc[a2] = row_acc[a2] + fr
+        col_acc[b2] = col_acc[b2] + fc
         for n in range(0, BLK, 16):
-            part = turned[n : n + 16]
-            dx = other[0:1] - part[:, 0:1]
-            dy = other[1:2] - part[:, 1:2]
-            dz = other[2:3] - part[:, 2:3]
-            sig = other[3:4] + part[:, 3:4]
-            well = other[4:5] * part[:, 4:5]
-            r2 = dx * dx + dy * dy + dz * dz
-            sig2 = sig * sig
-            soft = r2 + sig2
+            w = jnp.maximum(terms[n : n + 16, 0:BLK], 0.0)
+            soft = terms[n : n + 16, BLK : 2 * BLK]
+            sig2 = terms[n : n + 16, 2 * BLK : 3 * BLK]
             guess = pl.reciprocal(soft, approx=True)
             inv = guess * (2.0 - soft * guess)
             ratio = sig2 * inv
             u3 = ratio * ratio * ratio
-            w = jnp.maximum(1.0 - r2 * (1.0 / cutoff_sq), 0.0)
-            lead = (3.0 - 6.0 * u3) * (inv * w)
-            rest = (2.0 / cutoff_sq) - (2.0 / cutoff_sq) * u3
-            k = (lead + rest) * (u3 * w * well)
-            head = k.astype(jnp.bfloat16)
-            heads.append(head)
-            tails.append((k - head.astype(jnp.float32)).astype(jnp.bfloat16))
-        head, tail = jnp.concatenate(heads, axis=0), jnp.concatenate(tails, axis=0)
-        px, py = row_parts[a], col_parts[b]
-        across = (((1,), (1,)), ((), ()))
-        down = (((1,), (0,)), ((), ()))
-        vr = lax.dot_general(py, head, across, preferred_element_type=jnp.float32) + lax.dot_general(
-            py, tail, across, preferred_element_type=jnp.float32
-        )
-        vc = lax.dot_general(px, head, down, preferred_element_type=jnp.float32) + lax.dot_general(
-            px, tail, down, preferred_element_type=jnp.float32
-        )
-        vr, vc = vr[0:8] + vr[8:16], vc[0:8] + vc[8:16]
-        mine_r = px[0:8].astype(jnp.float32) + px[8:16].astype(jnp.float32)
-        theirs_r = py[0:8].astype(jnp.float32) + py[8:16].astype(jnp.float32)
-        fr = vr + (shift - mine_r) * vr[3:4]
-        fc = vc - (shift + theirs_r) * vc[3:4]
-        same = (b // BPD == row_id) & (a == col_id * BPD + b % BPD)
-        fc = fc * jnp.where(same, 0.0, 1.0)
-        on_row[a] = on_row[a] + fr[0:4]
-        on_col[b] = on_col[b] + fc[0:4]
-        return carry
-
-    lax.fori_loop(0, live[0], one_pair, 0)
+            t = inv * w
+            t1 = t + 1.0
+            k = (t1 - u3 * (t1 + t)) * (u3 * w)
+            high = k.astype(bf16)
+            k_head[n : n + 16, :] = high
+            k_tail[n : n + 16, :] = (k - high.astype(f32)).astype(bf16)
+        valid = p < total
+        q = jnp.minimum(p, BLK - 1)
+        a, b = jnp.where(valid, todo[0, q], NA), jnp.where(valid, todo[1, q], NB)
+        mine, theirs = rows[a], cols[b]
+        shift = wrap(col_mid[b] - row_mid[a])
+        other = theirs + shift
+        sq = mine * mine
+        norm = (sq[0:1] + sq[1:2] + sq[2:3]) * (1.0 / cutoff_sq)
+        left = jnp.where(
+            sub < 5, mine, jnp.where(sub == 5, norm, jnp.where(sub == 6, sq[3:4], 1.0))
+        )
+        head, mid, low = split3(left)
+        left = jnp.concatenate([head, head, head, mid, mid, low], axis=0).T.astype(bf16)
+        sq = other * other
+        norm = sq[0:1] + sq[1:2] + sq[2:3]
+        size2 = sq[3:4]
+        inv_c = 1.0 / scale
+        for_w = jnp.where(
+            sub < 3, other * (2.0 / cutoff_sq),
+            jnp.where(sub == 5, -1.0, jnp.where(sub == 7, 1.0 - norm * (1.0 / cutoff_sq), 0.0)),
+        )
+        for_sig = jnp.where(
+            sub == 3, other * (2.0 * inv_c), jnp.where(sub == 6, inv_c, jnp.where(sub == 7, size2 * inv_c, 0.0))
+        )
+        for_soft = jnp.where(
+            sub < 3, other * (-2.0 * inv_c),
+            jnp.where(sub == 5, cutoff_sq * inv_c, jnp.where(sub == 7, (norm + size2) * inv_c, for_sig)),
+        )
+        for n, right in enumerate((for_w, for_soft, for_sig)):
+            head, mid, low = split3(right)
+            right = jnp.concatenate([head, mid, low, head, mid, head], axis=0).astype(bf16)
+            terms[:, n * BLK : (n + 1) * BLK] = dot(left, right, down)
+        return a, b, a1, b1, shift, shift1
+
+    none = row_acc[0]
+    spare_a, spare_b = jnp.int32(NA), jnp.int32(NB)
+    lax.fori_loop(0, total + 2, turn, (spare_a, spare_b, spare_a, spare_b, none, none))
+    on_row[...] = row_acc[0:NA, 0:4, :]
+    on_col[...] = col_acc[0:NB, 0:4, :]
 
 
 def scatter_kernel(
-    on_row, on_col, old, vel, force, new_vel,
+    on_row, on_col, row_share, col_share,
     core_in, x_out, x_in, z_out, z_relay, z_in, y_in, zl_out, zl_in,
     send_sem, core_sem, x_sem, z_sem, y_sem, zl_sem,
 ):
@@ -316,20 +391,21 @@
     ship(z_out.at[me.z_far], z_in.at[0], z_sem.at[0], me.at_z(me.z_to))
     ship(z_out.at[me.z_from], z_in.at[1], z_sem.at[1], me.at_z(me.z_from))
 
-    result = zl_out[me.zl] + z_out[me.zh]
+    row_total, col_total = zl_out[me.zl], z_out[me.zh]
     for zl in me.zl_mates:
         arrived(zl_in.at[zl], zl_sem.at[zl])
-        result = result + zl_in[zl]
+        row_total = row_total + zl_in[zl]
+    for e in range(BPD):
+        row_share[:, BLK * e : BLK * (e + 1)] = row_total[e, 0:3]
     arrived(z_in.at[0], z_sem.at[0])
     z_relay[...] = z_in[0] + z_out[me.z_to]
     ship(z_relay, z_in.at[2], z_sem.at[2], me.at_z(me.z_to))
     arrived(z_in.at[1], z_sem.at[1])
-    result = result + z_in[1]
+    col_total = col_total + z_in[1]
     arrived(z_in.at[2], z_sem.at[2])
-    result = result + z_in[2]
+    col_total = col_total + z_in[2]
     for e in range(BPD):
-        force[:, BLK * e : BLK * (e + 1)] = result[e, 0:3]
-    new_vel[...] = vel[...] + 0.5 * time_step * (old[...] + force[...])
+        col_share[:, BLK * e : BLK * (e + 1)] = col_total[e, 0:3]
     for copy in started:
         copy.wait_send()
 
@@ -337,8 +413,7 @@
 def body(positions, velocities, old_forces, types, sigma_table, epsilon_table, pairs, live):
     f32 = jnp.float32
     dma = pltpu.SemaphoreType.DMA
-    moved = positions + time_step * velocities + 0.5 * time_step * time_step * old_forces
-    kinds = types.astype(f32).reshape(BPD, BLK)
+    kinds = types.reshape(BPD, BLK)
     vmem = pl.BlockSpec(memory_space=VMEM)
     smem = pl.BlockSpec(memory_space=pltpu.SMEM)
     row_group, col_group = pl.pallas_call(
@@ -357,28 +432,40 @@
     def pair_call(*refs):
         return pair_kernel(ROWS * cell_side, COLS * cell_side, *refs)
 
-    on_row, on_col = pl.pallas_call(
+    on_row, on_col, moved = pl.pallas_call(
         pair_call,
         out_shape=(
             jax.ShapeDtypeStruct((NA, 4, BLK), f32),
             jax.ShapeDtypeStruct((NB, 4, BLK), f32),
+            jax.ShapeDtypeStruct(positions.shape, f32),
         ),
-        in_specs=[smem] * 4 + [vmem] * 2,
-        out_specs=(vmem, vmem),
+        in_specs=[vmem] + [smem] * 3 + [vmem] * 5,
+        out_specs=(vmem, vmem, vmem),
         scratch_shapes=[
-            VMEM((NA, 8, BLK), f32),
-            VMEM((NB, 8, BLK), f32),
-            VMEM((NA, 16, BLK), jnp.bfloat16),
-            VMEM((NB, 16, BLK), jnp.bfloat16),
+            VMEM((NA + 1, 8, BLK), f32),
+            VMEM((NB + 1, 8, BLK), f32),
+            VMEM((NA + 1, 8, BLK), f32),
+            VMEM((NB + 1, 8, BLK), f32),
+            VMEM((NA + 1, 8, BLK), f32),
+            VMEM((NB + 1, 8, BLK), f32),
+            VMEM((8, BLK), jnp.int32),
+            pltpu.SMEM((8, BLK), jnp.int32),
+            VMEM((BLK, 3 * BLK), f32),
+            VMEM((BLK, BLK), jnp.bfloat16),
+            VMEM((BLK, BLK), jnp.bfloat16),
+            dma,
         ],
         name="pairs",
-    )(pairs.reshape(2, -1), live.reshape(1), sigma_table, epsilon_table, row_group, col_group)
+    )(
+        pairs.reshape(2, -1), live, sigma_table, epsilon_table, row_group, col_group,
+        positions, velocities, old_forces,
+    )
 
     tile = (BPD, 4, BLK)
-    new_forces, new_velocities = pl.pallas_call(
+    row_share, col_share = pl.pallas_call(
         scatter_kernel,
         out_shape=(jax.ShapeDtypeStruct(positions.shape, f32), jax.ShapeDtypeStruct(positions.shape, f32)),
-        in_specs=[vmem] * 4,
+        in_specs=[vmem] * 2,
         out_specs=(vmem, vmem),
         scratch_shapes=[
             VMEM((NX, NZH) + tile, f32),
@@ -402,9 +489,9 @@
     )(
         on_row.reshape((NZL, NY) + tile),
         on_col.reshape((NZH, NX, NK) + tile),
-        old_forces,
-        velocities,
     )
+    new_forces = row_share + col_share
+    new_velocities = velocities + 0.5 * time_step * (old_forces + new_forces)
     return moved, new_velocities, new_forces
 
 

time: 115 us -> 73.9 us (0.64)
  Pallas kernels: 108 us -> 70.2 us
  local copies, waits for them, and re-layouts: 1.39 us -> 0.01 us
    pallas_call x1, Pallas kernels: 43.8 us -> 20.4 us  [body(): pl.pallas_call(scatter_kernel, out_shape=(jax.ShapeDtypeStruct(positions....]
    pallas_call x1, Pallas kernels: 36.7 us -> 22.1 us  [body(): pl.pallas_call(pair_call, out_shape=(jax.ShapeDtypeStruct((NA, 4, BLK), f...]
    unnamed x12 -> x4, local copies, waits for them, and re-layouts: 1.39 us -> 0.01 us
    reshape x1 -> x0, other arithmetic: 1.26 us -> none  [body(): kinds = types.astype(f32).reshape(BPD, BLK)]
where the time goes in v2:
time: 73.9 us; the launch traced here: 72.9 us
  Pallas kernels  70.2 us (95%)
  between operations  1.33 us (2%)
  other arithmetic  1.32 us (2%)
    pallas_call x1, Pallas kernels, body(): pl.pallas_call(gather_kernel, out_shape=(jax.ShapeDtypeStruct((NA * 4, BL...  27.7 us
    pallas_call x1, Pallas kernels, body(): pl.pallas_call(pair_call, out_shape=(jax.ShapeDtypeStruct((NA, 4, BLK), f...  22.1 us
    pallas_call x1, Pallas kernels, body(): pl.pallas_call(scatter_kernel, out_shape=(jax.ShapeDtypeStruct(positions....  20.4 us

profile of v2, /device:TPU:6, one launch (start us, length us, event | category | flops | bytes accessed | tf_op | source)
XLA Modules:
  0.0 72.9 jit_solution(814229546091821145)
XLA Ops:
  1.3 27.7 %gather.1 = (f32[256,128]{1,0:T(8,128)}, f32[512,128]{1,0:T(8,128)}) custom-call(f32[3,512]{1,0:T(4,128)} %refs_6_.1, f32[3,512]{1,0:T(4,128)} %refs_7_.1, f32[3,512]{1,0:T(4,128)} %refs_8_.1, s32[4,128]{1,0:T(4,128)} %bitcast.6), custom_call_target="tpu_custom_call" | custom-call | tf_op jit(solution)/shard_map/gather/pallas_call | solution.py:419
  29.0 22.1 %pairs.1 = (f32[64,4,128]{2,1,0:T(4,128)}, f32[128,4,128]{2,1,0:T(4,128)}, f32[3,512]{1,0:T(4,128)}) custom-call(s32[2,128]{1,0:T(2,128)} %bitcast.7, s32[1,1]{1,0:T(1,128)S(6)} %copy.11.refs_1_, f32[18]{0:T(128)} %refs_2_.1, f32[18]{0:T(128)} %refs_3_.1, f32[256,128]{1,0:T(8,128)} %get-tuple-element.10.refs_4_, f32[512,128]{1,0:T(8,128)} %get-tuple-element.11.refs_5_, ...), custom_call_target="tpu_custom_call" | custom-call | tf_op jit(solution)/shard_map/pairs/pallas_call | solution.py:435
  51.1 0.0 copy-start
  51.1 0.0 copy-start.1
  51.1 20.4 %scatter.1 = (f32[3,512]{1,0:T(4,128)}, f32[3,512]{1,0:T(4,128)}) custom-call(f32[4,4,4,4,128]{4,3,2,1,0:T(4,128)} %bitcast.5, f32[4,4,2,4,4,128]{5,4,3,2,1,0:T(4,128)} %bitcast.4), custom_call_target="tpu_custom_call" | custom-call | tf_op jit(solution)/shard_map/scatter/pallas_call | solution.py:465
  71.5 0.0 copy-done
  71.5 0.0 copy-done.1
  71.5 1.3 %multiply_add_fusion = (f32[3,512]{1,0:T(4,128)}, f32[3,512]{1,0:T(4,128)}) fusion(f32[3,512]{1,0:T(4,128)S(1)} %copy-done, f32[3,512]{1,0:T(4,128)S(1)} %copy-done.1, f32[3,512]{1,0:T(4,128)} %get-tuple-element.15, f32[3,512]{1,0:T(4,128)} %get-tuple-element.16), kind=kLoop, calls=%fused_computation | loop fusion | flops 6144 | bytes 36864 | tf_op jit(solution)/shard_map/add | solution.py:494
Async XLA Ops:
  51.1 20.4 %copy-start = (f32[3,512]{1,0:T(4,128)S(1)}, f32[3,512]{1,0:T(4,128)}, u32[]{:S(2)}) copy-start(f32[3,512]{1,0:T(4,128)} %refs_7_.1) | copy-start | bytes 18436
  51.1 20.4 %copy-start.1 = (f32[3,512]{1,0:T(4,128)S(1)}, f32[3,512]{1,0:T(4,128)}, u32[]{:S(2)}) copy-start(f32[3,512]{1,0:T(4,128)} %refs_8_.1) | copy-start | bytes 18436

commit v3 on v2

--- a/solution.py
+++ b/solution.py
@@ -47,6 +47,9 @@
     def at_x(self, x):
         return (self.row_slot(self.zh, x, self.k), self.c)
 
+    def at_x_other(self, x):
+        return (self.row_slot(self.zh, x, 1 - self.k), self.c)
+
     def at_core(self):
         return (self.row_slot(self.zh, self.x, 1 - self.k), self.c)
 
@@ -60,6 +63,7 @@
         return (
             [self.at_z(self.z_from), self.at_z(self.z_to), self.at_core()]
             + [self.at_x(x) for x in self.x_mates]
+            + [self.at_x_other(x) for x in self.x_mates]
             + [self.at_zl(z) for z in self.zl_mates]
             + [self.at_y(y) for y in self.y_mates]
         )
@@ -72,10 +76,27 @@
     return barrier
 
 
-def gather_kernel(pos, vel, old, kind, row_group, col_group, mine, send_sem, row_sem, col_sem):
+def gather_kernel(
+    pos_hbm, vel_hbm, old_hbm, kind_hbm, sigma_hbm, epsilon_hbm, pairs_hbm, live_hbm,
+    row_group, col_group, moved, pairs, tables,
+    pos, vel, old, kind, sigma, epsilon, live, mine, local_sem, send_sem, row_sem, col_sem,
+):
     me = Place()
     barrier = greet(me)
-    moved = pos[...] + time_step * vel[...] + 0.5 * time_step * time_step * old[...]
+    local = [
+        pltpu.make_async_copy(src, dst, local_sem.at[n])
+        for n, (src, dst) in enumerate(
+            (
+                (pos_hbm, pos), (vel_hbm, vel), (old_hbm, old), (kind_hbm, kind),
+                (sigma_hbm, sigma), (epsilon_hbm, epsilon), (live_hbm, live), (pairs_hbm, pairs),
+            )
+        )
+    ]
+    for copy in local:
+        copy.start()
+    for copy in local[:4]:
+        copy.wait()
+    moved[...] = pos[...] + time_step * vel[...] + 0.5 * time_step * time_step * old[...]
     kinds = kind[...].astype(jnp.float32)
     for e in range(BPD):
         mine[4 * e : 4 * e + 3, :] = moved[:, BLK * e : BLK * (e + 1)]
@@ -122,13 +143,27 @@
         ship(mine, row_group, row_sem, me.c, me.at_y(y))
     ship(mine, col_group, col_sem, own_row, me.at_core())
 
-    def spread(zh, relay):
+    for copy in local[4:]:
+        copy.wait()
+    lane = lax.broadcasted_iota(jnp.int32, (8, BLK), 1)
+    sizes = jnp.zeros((8, BLK), jnp.float32)
+    wells = jnp.zeros((8, BLK), jnp.float32)
+    for n in range(sigma.shape[0]):
+        sizes = jnp.where(lane == n, 0.5 * sigma[n], sizes)
+        wells = jnp.where(lane == n, epsilon[n], wells)
+    tables[0] = sizes
+    tables[1] = math.sqrt(16.0 / cutoff_sq) * jnp.sqrt(wells)
+    tables[2] = jnp.full((8, BLK), live[0, 0].astype(jnp.float32))
+
+    def spread(zh, relay=False, last=False):
         slot = me.row_slot(zh, me.x, me.k)
         view = arrived(col_group, col_sem, slot)
         if relay:
             ship(view, col_group, col_sem, slot, me.at_z(me.z_to))
         for x in me.x_mates:
             ship(view, col_group, col_sem, slot, me.at_x(x))
+            if last:
+                ship(view, col_group, col_sem, slot, me.at_x_other(x))
         ship(view, col_group, col_sem, slot, me.at_core())
 
     def share(zh, x):
@@ -147,14 +182,14 @@
     for x in me.x_mates:
         share(me.zh, x)
     fan_out(me.zl_mates[0])
-    spread(me.z_from, True)
-    spread(me.z_to, False)
+    spread(me.z_from, relay=True)
+    spread(me.z_to)
     for x in me.x_mates:
         share(me.z_from, x)
         share(me.z_to, x)
-    spread(me.z_far, False)
+    spread(me.z_far, last=True)
     for x in me.x_mates:
-        share(me.z_far, x)
+        arrived(col_group, col_sem, me.row_slot(me.z_far, x, me.k))
     for y in me.y_mates:
         for zl in range(NZL):
             arrived(row_group, row_sem, me.col_slot(zl, y))
@@ -173,19 +208,16 @@
 
 
 def pair_kernel(
-    box_y, box_z, pairs, live, sigma, epsilon, row_group, col_group, pos, vel, old, on_row, on_col, moved,
-    rows, cols, row_mid, col_mid, row_acc, col_acc, listed, todo, terms, k_head, k_tail, sem,
+    box_y, box_z, pairs, tables, row_group, col_group, moved_in, on_row, on_col, moved,
+    rows, cols, row_mid, col_mid, row_acc, col_acc, listed, todo, k_parts, lefts, rights, sources, sem,
 ):
     f32, bf16 = jnp.float32, jnp.bfloat16
-    moved[...] = pos[...] + time_step * vel[...] + 0.5 * time_step * time_step * old[...]
+    moved[...] = moved_in[...]
+    row_acc[...] = jnp.zeros_like(row_acc)
+    col_acc[...] = jnp.zeros_like(col_acc)
     sub = lax.broadcasted_iota(jnp.int32, (8, BLK), 0)
     lane = lax.broadcasted_iota(jnp.int32, (8, BLK), 1)
-    sizes = jnp.zeros((8, BLK), f32)
-    wells = jnp.zeros((8, BLK), f32)
-    for n in range(sigma.shape[0]):
-        sizes = jnp.where(lane == n, 0.5 * sigma[n], sizes)
-        wells = jnp.where(lane == n, epsilon[n], wells)
-    wells = math.sqrt(16.0 / cutoff_sq) * jnp.sqrt(wells)
+    sizes, wells = tables[0], tables[1]
     kind_row = (sub == 3) | (sub == 7)
     box = jnp.where(sub == 0, BPD * cell_side, jnp.where(sub == 1, box_y, jnp.where(sub == 2, box_z, 1.0)))
     inverse_box = 1.0 / box
@@ -214,7 +246,7 @@
             return jnp.where(here, low, bounds[0]), jnp.where(here, high, bounds[1])
 
         start = group[0:8, :]
-        return lax.fori_loop(0, group.shape[0] // 8, two_blocks, (start, start), unroll=4)
+        return lax.fori_loop(0, group.shape[0] // 8, two_blocks, (start, start), unroll=8)
 
     row_low, row_high = prepare(row_group, rows, row_mid)
     col_low, col_high = prepare(col_group, cols, col_mid)
@@ -233,7 +265,7 @@
     gap = jnp.where(sub < 3, jnp.maximum(gap, 0.0), 0.0)
     gap2 = jnp.sum(gap * gap, axis=0, keepdims=True)
     near_by = jnp.broadcast_to(gap2, (8, BLK)) < cutoff_sq + 0.01
-    active = jnp.where(near_by & (lane < live[0, 0]), 1.0, 0.0)
+    active = jnp.where(near_by & (lane.astype(f32) < tables[2]), 1.0, 0.0)
     big_sub = lax.broadcasted_iota(jnp.int32, (BLK, BLK), 0)
     big_lane = lax.broadcasted_iota(jnp.int32, (BLK, BLK), 1)
     across = (((1,), (1,)), ((), ()))
@@ -254,8 +286,6 @@
     listed[...] = jnp.where(sub == 2, count, packed).astype(jnp.int32)
     copy = pltpu.make_async_copy(listed, todo, sem)
     copy.start()
-    row_acc[...] = jnp.zeros_like(row_acc)
-    col_acc[...] = jnp.zeros_like(col_acc)
     copy.wait()
     total = todo[2, 0]
     row_id, col_id = lax.axis_index("row"), lax.axis_index("col")
@@ -272,23 +302,31 @@
         v = v[0:8] + v[8:16]
         return v + pltpu.roll(v, 4, 0)
 
-    def turn(p, carry):
-        a1, b1, a2, b2, shift1, shift2 = carry
-        mine, theirs = rows[a2], cols[b2]
-        px, py = force_sources(mine), force_sources(theirs)
-        head, tail = k_head[...], k_tail[...]
-        vr = fold(dot(py, head, across) + dot(py, tail, across))
-        vc = fold(dot(px, head, down) + dot(px, tail, down))
-        fr = (vr + (shift2 - mine) * vr[3:4]) * mine[4:5]
-        fc = (vc - (shift2 + theirs) * vc[3:4]) * theirs[4:5]
-        same = (b2 // BPD == row_id) & (a2 == col_id * BPD + b2 % BPD)
+    def entry(p):
+        valid = (p >= 0) & (p < total)
+        q = jnp.clip(p, 0, BLK - 1)
+        return jnp.where(valid, todo[0, q], NA), jnp.where(valid, todo[1, q], NB)
+
+    def finish(n, p, vr, vc):
+        a, b = entry(p)
+        mine, theirs = rows[a], cols[b]
+        shift = wrap(col_mid[b] - row_mid[a])
+        vr, vc = fold(vr), fold(vc)
+        fr = (vr + (shift - mine) * vr[3:4]) * mine[4:5]
+        fc = (vc - (shift + theirs) * vc[3:4]) * theirs[4:5]
+        same = (b // BPD == row_id) & (a == col_id * BPD + b % BPD)
         fc = fc * jnp.where(same, 0.0, 1.0)
-        row_acc[a2] = row_acc[a2] + fr
-        col_acc[b2] = col_acc[b2] + fc
-        for n in range(0, BLK, 16):
-            w = jnp.maximum(terms[n : n + 16, 0:BLK], 0.0)
-            soft = terms[n : n + 16, BLK : 2 * BLK]
-            sig2 = terms[n : n + 16, 2 * BLK : 3 * BLK]
+        row_acc[a] = row_acc[a] + fr
+        col_acc[b] = col_acc[b] + fc
+
+    def pull(n, head, tail):
+        px, py = sources[n, 0], sources[n, 1]
+        return dot(py, head, across) + dot(py, tail, across), dot(px, head, down) + dot(px, tail, down)
+
+    def coefficients(n, p, terms):
+        for m in range(0, BLK, 16):
+            w, soft, sig2 = [v[m : m + 16] for v in terms]
+            w = jnp.maximum(w, 0.0)
             guess = pl.reciprocal(soft, approx=True)
             inv = guess * (2.0 - soft * guess)
             ratio = sig2 * inv
@@ -297,21 +335,21 @@
             t1 = t + 1.0
             k = (t1 - u3 * (t1 + t)) * (u3 * w)
             high = k.astype(bf16)
-            k_head[n : n + 16, :] = high
-            k_tail[n : n + 16, :] = (k - high.astype(f32)).astype(bf16)
-        valid = p < total
-        q = jnp.minimum(p, BLK - 1)
-        a, b = jnp.where(valid, todo[0, q], NA), jnp.where(valid, todo[1, q], NB)
+            k_parts[n, 0, m : m + 16, :] = high
+            k_parts[n, 1, m : m + 16, :] = (k - high.astype(f32)).astype(bf16)
+        a, b = entry(p)
+        sources[n, 0] = force_sources(rows[a])
+        sources[n, 1] = force_sources(cols[b])
+
+    def describe(n, p):
+        a, b = entry(p)
         mine, theirs = rows[a], cols[b]
-        shift = wrap(col_mid[b] - row_mid[a])
-        other = theirs + shift
+        other = theirs + wrap(col_mid[b] - row_mid[a])
         sq = mine * mine
         norm = (sq[0:1] + sq[1:2] + sq[2:3]) * (1.0 / cutoff_sq)
-        left = jnp.where(
-            sub < 5, mine, jnp.where(sub == 5, norm, jnp.where(sub == 6, sq[3:4], 1.0))
-        )
+        left = jnp.where(sub < 5, mine, jnp.where(sub == 5, norm, jnp.where(sub == 6, sq[3:4], 1.0)))
         head, mid, low = split3(left)
-        left = jnp.concatenate([head, head, head, mid, mid, low], axis=0).T.astype(bf16)
+        lefts[n] = jnp.concatenate([head, head, head, mid, mid, low], axis=0).T.astype(bf16)
         sq = other * other
         norm = sq[0:1] + sq[1:2] + sq[2:3]
         size2 = sq[3:4]
@@ -327,23 +365,30 @@
             sub < 3, other * (-2.0 * inv_c),
             jnp.where(sub == 5, cutoff_sq * inv_c, jnp.where(sub == 7, (norm + size2) * inv_c, for_sig)),
         )
-        for n, right in enumerate((for_w, for_soft, for_sig)):
+        for m, right in enumerate((for_w, for_soft, for_sig)):
             head, mid, low = split3(right)
-            right = jnp.concatenate([head, mid, low, head, mid, head], axis=0).astype(bf16)
-            terms[:, n * BLK : (n + 1) * BLK] = dot(left, right, down)
-        return a, b, a1, b1, shift, shift1
-
-    none = row_acc[0]
-    spare_a, spare_b = jnp.int32(NA), jnp.int32(NB)
-    lax.fori_loop(0, total + 2, turn, (spare_a, spare_b, spare_a, spare_b, none, none))
+            rights[n, m] = jnp.concatenate([head, mid, low, head, mid, head], axis=0).astype(bf16)
+
+    def turn(g, carry):
+        held = [(k_parts[n, 0], k_parts[n, 1]) for n in range(4)]
+        terms = [[dot(lefts[n], rights[n, m], down) for m in range(3)] for n in range(4)]
+        for n in range(4):
+            finish(n, 4 * (g - 2) + n, *pull(n, *held[n]))
+        for n in range(4):
+            coefficients(n, 4 * (g - 1) + n, terms[n])
+        for n in range(4):
+            describe(n, 4 * g + n)
+        return carry
+
+    lax.fori_loop(0, (total + 4 - 1) // 4 + 2, turn, 0)
     on_row[...] = row_acc[0:NA, 0:4, :]
     on_col[...] = col_acc[0:NB, 0:4, :]
 
 
 def scatter_kernel(
     on_row, on_col, row_share, col_share,
-    core_in, x_out, x_in, z_out, z_relay, z_in, y_in, zl_out, zl_in,
-    send_sem, core_sem, x_sem, z_sem, y_sem, zl_sem,
+    far_in, far_out, core_in, near_out, near_in, near_sum, z_relay, z_in, y_in, zl_out, zl_in,
+    send_sem, far_sem, core_sem, near_sem, z_sem, y_sem, zl_sem,
 ):
     me = Place()
     barrier = greet(me)
@@ -364,42 +409,60 @@
             device_id=me.at_core(), device_id_type=MESH,
         ).wait_recv()
 
-    xs = me.x_mates + [me.x]
-    for x in xs:
-        ship(on_col.at[:, x, 1 - me.k], core_in.at[x], core_sem.at[x], me.at_core())
+    def far(x, k, device):
+        ship(on_col.at[me.z_far, x, k], far_in.at[me.x * NK + me.k], far_sem.at[me.x * NK + me.k], device)
+
+    for x in me.x_mates:
+        far(x, me.k, me.at_x(x))
+        far(x, 1 - me.k, me.at_x_other(x))
+    far(me.x, 1 - me.k, me.at_core())
+    near = [(me.zh + 3) % NZH, me.zh, (me.zh + 1) % NZH]
+    j_from, j_to = 2 * me.k, 2 - 2 * me.k
+    for j, zh in enumerate(near):
+        ship(on_col.at[zh, :, 1 - me.k], core_in.at[j], core_sem.at[j], me.at_core())
     for y in me.y_mates:
         ship(on_row.at[:, y], y_in.at[me.y], y_sem.at[me.y], me.at_y(y))
+    for j, zh in enumerate(near):
+        arrived(core_in.at[j], core_sem.at[j])
+        for x in me.x_mates:
+            near_out[x, j] = on_col[zh, x, me.k] + core_in[j, x]
+        near_sum[j] = on_col[zh, me.x, me.k] + core_in[j, me.x]
     for x in me.x_mates:
-        arrived(core_in.at[x], core_sem.at[x])
-        x_out[x] = on_col[:, x, me.k] + core_in[x]
-        ship(x_out.at[x], x_in.at[me.x], x_sem.at[me.x], me.at_x(x))
-    arrived(core_in.at[me.x], core_sem.at[me.x])
-    own = on_col[:, me.x, me.k] + core_in[me.x]
+        ship(near_out.at[x], near_in.at[me.x], near_sem.at[me.x], me.at_x(x))
+    total = on_col[me.z_far, me.x, me.k]
+    order = [(me.x, 1 - me.k)]
+    for x in (me.x_mates[1], me.x_mates[2], me.x_mates[0]):
+        order += [(x, me.k), (x, 1 - me.k)]
+    for x, k in order:
+        arrived(far_in.at[x * NK + k], far_sem.at[x * NK + k])
+        total = total + far_in[x * NK + k]
+    far_out[...] = total
+    ship(far_out, z_in.at[0], z_sem.at[0], me.at_z(me.z_to))
+
+    for x in (me.x_mates[1], me.x_mates[2], me.x_mates[0]):
+        arrived(near_in.at[x], near_sem.at[x])
+    near_sum[...] = (
+        near_sum[...] + near_in[me.x_mates[0]] + near_in[me.x_mates[1]] + near_in[me.x_mates[2]]
+    )
+    ship(near_sum.at[j_from], z_in.at[1], z_sem.at[1], me.at_z(me.z_from))
 
     total = on_row[:, me.y]
-    for y in (me.y_mates[1], me.y_mates[2], me.y_mates[0]):
+    for y in me.y_mates:
         arrived(y_in.at[y], y_sem.at[y])
         total = total + y_in[y]
     zl_out[...] = total
     for zl in me.zl_mates:
         ship(zl_out.at[zl], zl_in.at[me.zl], zl_sem.at[me.zl], me.at_zl(zl))
 
-    for x in (me.x_mates[1], me.x_mates[2], me.x_mates[0]):
-        arrived(x_in.at[x], x_sem.at[x])
-        own = own + x_in[x]
-    z_out[...] = own
-    ship(z_out.at[me.z_far], z_in.at[0], z_sem.at[0], me.at_z(me.z_to))
-    ship(z_out.at[me.z_from], z_in.at[1], z_sem.at[1], me.at_z(me.z_from))
-
-    row_total, col_total = zl_out[me.zl], z_out[me.zh]
+    arrived(z_in.at[0], z_sem.at[0])
+    z_relay[...] = z_in[0] + near_sum[j_to]
+    ship(z_relay, z_in.at[2], z_sem.at[2], me.at_z(me.z_to))
+    row_total, col_total = zl_out[me.zl], near_sum[1]
     for zl in me.zl_mates:
         arrived(zl_in.at[zl], zl_sem.at[zl])
         row_total = row_total + zl_in[zl]
     for e in range(BPD):
         row_share[:, BLK * e : BLK * (e + 1)] = row_total[e, 0:3]
-    arrived(z_in.at[0], z_sem.at[0])
-    z_relay[...] = z_in[0] + z_out[me.z_to]
-    ship(z_relay, z_in.at[2], z_sem.at[2], me.at_z(me.z_to))
     arrived(z_in.at[1], z_sem.at[1])
     col_total = col_total + z_in[1]
     arrived(z_in.at[2], z_sem.at[2])
@@ -413,21 +476,47 @@
 def body(positions, velocities, old_forces, types, sigma_table, epsilon_table, pairs, live):
     f32 = jnp.float32
     dma = pltpu.SemaphoreType.DMA
-    kinds = types.reshape(BPD, BLK)
     vmem = pl.BlockSpec(memory_space=VMEM)
-    smem = pl.BlockSpec(memory_space=pltpu.SMEM)
-    row_group, col_group = pl.pallas_call(
+    hbm = pl.BlockSpec(memory_space=pltpu.HBM)
+    i32 = jnp.int32
+    coords = positions.shape
+    row_group, col_group, moved_near, pairs_near, tables = pl.pallas_call(
         gather_kernel,
         out_shape=(
             jax.ShapeDtypeStruct((NA * 4, BLK), f32),
             jax.ShapeDtypeStruct((NB * 4, BLK), f32),
+            jax.ShapeDtypeStruct(coords, f32),
+            jax.ShapeDtypeStruct((2, BLK), i32),
+            jax.ShapeDtypeStruct((3, 8, BLK), f32),
         ),
-        in_specs=[vmem] * 4,
-        out_specs=(vmem, vmem),
-        scratch_shapes=[VMEM((4 * BPD, BLK), f32), dma((48,)), dma((COLS,)), dma((ROWS,))],
-        compiler_params=pltpu.CompilerParams(collective_id=0, has_side_effects=True),
+        in_specs=[hbm] * 8,
+        out_specs=(vmem,) * 5,
+        scratch_shapes=[
+            VMEM(coords, f32),
+            VMEM(coords, f32),
+            VMEM(coords, f32),
+            VMEM((BPD, BLK), i32),
+            pltpu.SMEM(sigma_table.shape, f32),
+            pltpu.SMEM(epsilon_table.shape, f32),
+            pltpu.SMEM((1, 1), i32),
+            VMEM((4 * BPD, BLK), f32),
+            dma((8,)),
+            dma((48,)),
+            dma((COLS,)),
+            dma((ROWS,)),
+        ],
+        compiler_params=pltpu.CompilerParams(collective_id=0, has_side_effects=True, vmem_limit_bytes=8 << 20),
         name="gather",
-    )(positions, velocities, old_forces, kinds)
+    )(
+        *[
+            pltpu.with_memory_space_constraint(v, pltpu.HBM)
+            for v in (
+                positions, velocities, old_forces, types.reshape(BPD, BLK), sigma_table, epsilon_table,
+                pairs.reshape(2, BLK),
+            )
+        ],
+        live,
+    )
 
     def pair_call(*refs):
         return pair_kernel(ROWS * cell_side, COLS * cell_side, *refs)
@@ -439,7 +528,7 @@
             jax.ShapeDtypeStruct((NB, 4, BLK), f32),
             jax.ShapeDtypeStruct(positions.shape, f32),
         ),
-        in_specs=[vmem] + [smem] * 3 + [vmem] * 5,
+        in_specs=[vmem] * 5,
         out_specs=(vmem, vmem, vmem),
         scratch_shapes=[
             VMEM((NA + 1, 8, BLK), f32),
@@ -450,15 +539,16 @@
             VMEM((NB + 1, 8, BLK), f32),
             VMEM((8, BLK), jnp.int32),
             pltpu.SMEM((8, BLK), jnp.int32),
-            VMEM((BLK, 3 * BLK), f32),
-            VMEM((BLK, BLK), jnp.bfloat16),
-            VMEM((BLK, BLK), jnp.bfloat16),
+            VMEM((4, 2, BLK, BLK), jnp.bfloat16),
+            VMEM((4, BLK, 48), jnp.bfloat16),
+            VMEM((4, 3, 48, BLK), jnp.bfloat16),
+            VMEM((4, 2, 16, BLK), jnp.bfloat16),
             dma,
         ],
+        compiler_params=pltpu.CompilerParams(vmem_limit_bytes=16 << 20),
         name="pairs",
     )(
-        pairs.reshape(2, -1), live, sigma_table, epsilon_table, row_group, col_group,
-        positions, velocities, old_forces,
+        pairs_near, tables, row_group, col_group, moved_near,
     )
 
     tile = (BPD, 4, BLK)
@@ -468,23 +558,26 @@
         in_specs=[vmem] * 2,
         out_specs=(vmem, vmem),
         scratch_shapes=[
-            VMEM((NX, NZH) + tile, f32),
-            VMEM((NX, NZH) + tile, f32),
-            VMEM((NX, NZH) + tile, f32),
-            VMEM((NZH,) + tile, f32),
+            VMEM((NX * NK,) + tile, f32),
+            VMEM(tile, f32),
+            VMEM((3, NX) + tile, f32),
+            VMEM((NX, 3) + tile, f32),
+            VMEM((NX, 3) + tile, f32),
+            VMEM((3,) + tile, f32),
             VMEM(tile, f32),
             VMEM((3,) + tile, f32),
             VMEM((NY, NZL) + tile, f32),
             VMEM((NZL,) + tile, f32),
             VMEM((NZL,) + tile, f32),
-            dma((16,)),
-            dma((NX,)),
+            dma((24,)),
+            dma((NX * NK,)),
+            dma((3,)),
             dma((NX,)),
             dma((3,)),
             dma((NY,)),
             dma((NZL,)),
         ],
-        compiler_params=pltpu.CompilerParams(collective_id=1, has_side_effects=True),
+        compiler_params=pltpu.CompilerParams(collective_id=1, has_side_effects=True, vmem_limit_bytes=8 << 20),
         name="scatter",
     )(
         on_row.reshape((NZL, NY) + tile),

time: 73.9 us -> 58.5 us (0.79)
  Pallas kernels: 70.2 us -> 55.7 us
    pallas_call x1, Pallas kernels: 22.1 us -> 12.6 us  [body(): pl.pallas_call(pair_call, out_shape=(jax.ShapeDtypeStruct((NA, 4, BLK), f...]
    pallas_call x1, Pallas kernels: 20.4 us -> 17.2 us  [body(): pl.pallas_call(scatter_kernel, out_shape=(jax.ShapeDtypeStruct(positions....]
    pallas_call x1, Pallas kernels: 27.7 us -> 25.8 us  [body(): pl.pallas_call(gather_kernel, out_shape=(jax.ShapeDtypeStruct((NA * 4, BL...]
where the time goes in v3:
time: 58.5 us; the launch traced here: 57.6 us
  Pallas kernels  55.7 us (95%)
  between operations  1.33 us (2%)
  other arithmetic  0.61 us (1%)
    pallas_call x1, Pallas kernels, body(): pl.pallas_call(gather_kernel, out_shape=(jax.ShapeDtypeStruct((NA * 4, BL...  25.8 us
    pallas_call x1, Pallas kernels, body(): pl.pallas_call(scatter_kernel, out_shape=(jax.ShapeDtypeStruct(positions....  17.2 us
    pallas_call x1, Pallas kernels, body(): pl.pallas_call(pair_call, out_shape=(jax.ShapeDtypeStruct((NA, 4, BLK), f...  12.6 us

profile of v3, /device:TPU:6, one launch (start us, length us, event | category | flops | bytes accessed | tf_op | source)
XLA Modules:
  0.0 57.6 jit_solution(15460281428302742610)
XLA Ops:
  1.3 25.8 %gather.1 = (f32[256,128]{1,0:T(8,128)S(1)}, f32[512,128]{1,0:T(8,128)S(1)}, f32[3,512]{1,0:T(4,128)S(1)}, s32[2,128]{1,0:T(2,128)S(1)}, f32[3,8,128]{2,1,0:T(8,128)S(1)}) custom-call(f32[3,512]{1,0:T(4,128)} %pos_hbm.1, f32[3,512]{1,0:T(4,128)} %vel_hbm.1, f32[3,512]{1,0:T(4,128)} %old_hbm.1, s32[4,128]{1,0:T(4,128)} %bitcast.6, f32[18]{0:T(128)} %sigma_hbm.1, ...), custom_call_target="tpu_custom_call" | custom-call | tf_op jit(solution)/shard_map/gather/pallas_call | solution.py:483
  27.1 12.6 %pairs.1 = (f32[64,4,128]{2,1,0:T(4,128)S(1)}, f32[128,4,128]{2,1,0:T(4,128)S(1)}, f32[3,512]{1,0:T(4,128)}) custom-call(s32[2,128]{1,0:T(2,128)S(1)} %get-tuple-element.13.refs_0_, f32[3,8,128]{2,1,0:T(8,128)S(1)} %get-tuple-element.14.refs_1_, f32[256,128]{1,0:T(8,128)S(1)} %get-tuple-element.15.refs_2_, f32[512,128]{1,0:T(8,128)S(1)} %get-tuple-element.16.refs_3_, ...), custom_call_target="tpu_custom_call" | custom-call | tf_op jit(solution)/shard_map/pairs/pallas_call | solution.py:524
  39.7 0.0 copy-start
  39.7 0.0 copy-start.1
  39.7 17.2 %scatter.1 = (f32[3,512]{1,0:T(4,128)S(1)}, f32[3,512]{1,0:T(4,128)S(1)}) custom-call(f32[4,4,4,4,128]{4,3,2,1,0:T(4,128)S(1)} %bitcast.5, f32[4,4,2,4,4,128]{5,4,3,2,1,0:T(4,128)S(1)} %bitcast.4), custom_call_target="tpu_custom_call" | custom-call | tf_op jit(solution)/shard_map/scatter/pallas_call | solution.py:555
  57.0 0.0 copy-done
  57.0 0.0 copy-done.1
  57.0 0.6 %multiply_add_fusion = (f32[3,512]{1,0:T(4,128)}, f32[3,512]{1,0:T(4,128)}) fusion(f32[3,512]{1,0:T(4,128)S(1)} %copy-done, f32[3,512]{1,0:T(4,128)S(1)} %copy-done.1, f32[3,512]{1,0:T(4,128)S(1)} %get-tuple-element.21, f32[3,512]{1,0:T(4,128)S(1)} %get-tuple-element.22), kind=kLoop, calls=%fused_computation | loop fusion | flops 6144 | bytes 36864 | tf_op jit(solution)/shard_map/add | solution.py:587
Async XLA Ops:
  39.7 17.3 %copy-start = (f32[3,512]{1,0:T(4,128)S(1)}, f32[3,512]{1,0:T(4,128)}, u32[]{:S(2)}) copy-start(f32[3,512]{1,0:T(4,128)} %vel_hbm.1) | copy-start | bytes 18436
  39.7 17.3 %copy-start.1 = (f32[3,512]{1,0:T(4,128)S(1)}, f32[3,512]{1,0:T(4,128)}, u32[]{:S(2)}) copy-start(f32[3,512]{1,0:T(4,128)} %old_hbm.1) | copy-start | bytes 18436

commit v4 on v3

--- a/solution.py
+++ b/solution.py
@@ -78,7 +78,7 @@
 
 def gather_kernel(
     pos_hbm, vel_hbm, old_hbm, kind_hbm, sigma_hbm, epsilon_hbm, pairs_hbm, live_hbm,
-    row_group, col_group, moved, pairs, tables,
+    row_group, col_group, moved, pairs, tables, row_mid, col_mid, row_ends, col_ends,
     pos, vel, old, kind, sigma, epsilon, live, mine, local_sem, send_sem, row_sem, col_sem,
 ):
     me = Place()
@@ -177,25 +177,65 @@
         for y in me.y_mates:
             ship(view, row_group, row_sem, slot, me.at_y(y))
 
+    def bound(group, middle, ends, slots):
+        found = []
+        for slot in slots:
+            for h in range(2):
+                both = group[pl.ds(pl.multiple_of(slot * 16 + 8 * h, 8), 8), :]
+                low = jnp.broadcast_to(jnp.min(both, axis=1, keepdims=True), (8, BLK))
+                high = jnp.broadcast_to(jnp.max(both, axis=1, keepdims=True), (8, BLK))
+                middle[2 * slot + h] = 0.5 * (low + high)
+                found.append((lane == 2 * slot + h, low, high))
+        lows, highs = ends[0], ends[1]
+        for here, low, high in found:
+            lows = jnp.where(here, low, lows)
+            highs = jnp.where(here, high, highs)
+        ends[0], ends[1] = lows, highs
+
+    def bound_rows(slots):
+        bound(row_group, row_mid, row_ends, slots)
+
+    def bound_cols(slots):
+        bound(col_group, col_mid, col_ends, slots)
+
+    def take_rows(slots):
+        for slot in slots:
+            arrived(row_group, row_sem, slot)
+        bound_rows(slots)
+
+    def take_cols(slots):
+        for slot in slots:
+            arrived(col_group, col_sem, slot)
+        bound_cols(slots)
+
+    for ends in (row_ends, col_ends):
+        ends[...] = jnp.zeros_like(ends)
+    bound_rows([me.c])
+    bound_cols([own_row])
     for zl in me.zl_mates[1:]:
         fan_out(zl)
     for x in me.x_mates:
         share(me.zh, x)
     fan_out(me.zl_mates[0])
+    bound_rows([me.col_slot(zl, me.y) for zl in me.zl_mates])
+    bound_cols([me.row_slot(me.zh, x, me.k) for x in me.x_mates])
     spread(me.z_from, relay=True)
     spread(me.z_to)
+    ends_z = (me.z_from, me.z_to)
+    bound_cols([me.row_slot(zh, me.x, me.k) for zh in ends_z])
+    xs = [me.x] + me.x_mates
+    take_cols([me.row_slot(me.zh, x, 1 - me.k) for x in xs])
+    take_rows([me.col_slot(me.zl, y) for y in me.y_mates])
     for x in me.x_mates:
         share(me.z_from, x)
         share(me.z_to, x)
+    bound_cols([me.row_slot(zh, x, me.k) for x in me.x_mates for zh in ends_z])
+    take_rows([me.col_slot(zl, y) for zl in me.zl_mates for y in me.y_mates])
     spread(me.z_far, last=True)
-    for x in me.x_mates:
-        arrived(col_group, col_sem, me.row_slot(me.z_far, x, me.k))
-    for y in me.y_mates:
-        for zl in range(NZL):
-            arrived(row_group, row_sem, me.col_slot(zl, y))
-    for zh in range(NZH):
-        for x in range(NX):
-            arrived(col_group, col_sem, me.row_slot(zh, x, 1 - me.k))
+    take_cols([me.row_slot(zh, x, 1 - me.k) for x in xs for zh in ends_z])
+    bound_cols([me.row_slot(me.z_far, me.x, me.k)])
+    take_cols([me.row_slot(me.z_far, me.x, 1 - me.k)])
+    take_cols([me.row_slot(me.z_far, x, k) for x in me.x_mates for k in (me.k, 1 - me.k)])
     for copy in started:
         copy.wait_send()
 
@@ -208,8 +248,8 @@
 
 
 def pair_kernel(
-    box_y, box_z, pairs, tables, row_group, col_group, moved_in, on_row, on_col, moved,
-    rows, cols, row_mid, col_mid, row_acc, col_acc, listed, todo, k_parts, lefts, rights, sources, sem,
+    box_y, box_z, pairs, tables, row_group, col_group, row_mid, col_mid, row_ends, col_ends, moved_in,
+    on_row, on_col, moved, rows, cols, row_acc, col_acc, listed, todo, k_parts, lefts, rights, sources, shifts, sem,
 ):
     f32, bf16 = jnp.float32, jnp.bfloat16
     moved[...] = moved_in[...]
@@ -225,31 +265,19 @@
     def wrap(v):
         return v - box * jnp.floor(v * inverse_box + 0.5)
 
-    def prepare(group, table, middle):
-        def two_blocks(g, bounds):
-            both = group[pl.ds(pl.multiple_of(8 * g, 8), 8), :]
-            low = jnp.broadcast_to(jnp.min(both, axis=1, keepdims=True), (8, BLK))
-            high = jnp.broadcast_to(jnp.max(both, axis=1, keepdims=True), (8, BLK))
-            center = 0.5 * (low + high)
-            near = both - center
-            kinds = jnp.where(kind_row, both, 0.0).astype(jnp.int32)
-            size = jnp.take_along_axis(sizes, kinds, axis=1, mode="promise_in_bounds")
-            well = pltpu.roll(jnp.take_along_axis(wells, kinds, axis=1, mode="promise_in_bounds"), 1, 0)
-            mixed = jnp.where(kind_row, size, near)
-            for h in range(2):
-                part = mixed if h == 0 else pltpu.roll(mixed, 4, 0)
-                deep = well if h == 0 else pltpu.roll(well, 4, 0)
-                mid = center if h == 0 else pltpu.roll(center, 4, 0)
-                table[2 * g + h] = jnp.where(sub < 4, part, jnp.where(sub == 4, deep, 0.0))
-                middle[2 * g + h] = jnp.where(sub < 3, mid, 0.0)
-            here = lane == g
-            return jnp.where(here, low, bounds[0]), jnp.where(here, high, bounds[1])
-
-        start = group[0:8, :]
-        return lax.fori_loop(0, group.shape[0] // 8, two_blocks, (start, start), unroll=8)
-
-    row_low, row_high = prepare(row_group, rows, row_mid)
-    col_low, col_high = prepare(col_group, cols, col_mid)
+    def look_up(group, middle, index):
+        g = index // 2
+        mid = middle[g]
+        both = group[pl.ds(pl.multiple_of(8 * g, 8), 8), :]
+        odd = jnp.full((8, BLK), index % 2) == 1
+        near = jnp.where(kind_row, both, both - mid)
+        near = jnp.where(odd, pltpu.roll(near, 4, 0), near)
+        mid = jnp.where(sub < 3, jnp.where(odd, pltpu.roll(mid, 4, 0), mid), 0.0)
+        kinds = jnp.broadcast_to(near[3:4], (8, BLK)).astype(jnp.int32)
+        size = jnp.take_along_axis(sizes, kinds, axis=1, mode="promise_in_bounds")
+        well = jnp.take_along_axis(wells, kinds, axis=1, mode="promise_in_bounds")
+        tile = jnp.where(sub < 3, near, jnp.where(sub == 3, size, jnp.where(sub == 4, well, 0.0)))
+        return tile, mid
 
     firsts = jnp.broadcast_to(pairs[0:1, :], (8, BLK))
     seconds = jnp.broadcast_to(pairs[1:2, :], (8, BLK))
@@ -258,8 +286,8 @@
         got = jnp.take_along_axis(bound, index >> 1, axis=1, mode="promise_in_bounds")
         return jnp.where((index & 1) == 1, pltpu.roll(got, 4, 0), got)
 
-    xl, xh = pick(row_low, firsts), pick(row_high, firsts)
-    yl, yh = pick(col_low, seconds), pick(col_high, seconds)
+    xl, xh = pick(row_ends[0], firsts), pick(row_ends[1], firsts)
+    yl, yh = pick(col_ends[0], seconds), pick(col_ends[1], seconds)
     apart = wrap(jnp.where(sub < 3, 0.5 * ((yl + yh) - (xl + xh)), 0.0))
     gap = jnp.abs(apart) - 0.5 * ((yh - yl) + (xh - xl))
     gap = jnp.where(sub < 3, jnp.maximum(gap, 0.0), 0.0)
@@ -310,7 +338,7 @@
     def finish(n, p, vr, vc):
         a, b = entry(p)
         mine, theirs = rows[a], cols[b]
-        shift = wrap(col_mid[b] - row_mid[a])
+        shift = shifts[p + 4]
         vr, vc = fold(vr), fold(vc)
         fr = (vr + (shift - mine) * vr[3:4]) * mine[4:5]
         fc = (vc - (shift + theirs) * vc[3:4]) * theirs[4:5]
@@ -321,11 +349,15 @@
 
     def pull(n, head, tail):
         px, py = sources[n, 0], sources[n, 1]
-        return dot(py, head, across) + dot(py, tail, across), dot(px, head, down) + dot(px, tail, down)
+        px, py = jnp.concatenate([px, px], axis=1), jnp.concatenate([py, py], axis=1)
+        return (
+            dot(py, jnp.concatenate([head, tail], axis=1), across),
+            dot(px, jnp.concatenate([head, tail], axis=0), down),
+        )
 
     def coefficients(n, p, terms):
         for m in range(0, BLK, 16):
-            w, soft, sig2 = [v[m : m + 16] for v in terms]
+            w, soft, sig2 = [terms[m : m + 16, BLK * v : BLK * (v + 1)] for v in range(3)]
             w = jnp.maximum(w, 0.0)
             guess = pl.reciprocal(soft, approx=True)
             inv = guess * (2.0 - soft * guess)
@@ -343,8 +375,13 @@
 
     def describe(n, p):
         a, b = entry(p)
-        mine, theirs = rows[a], cols[b]
-        other = theirs + wrap(col_mid[b] - row_mid[a])
+        mine, near_mid = look_up(row_group, row_mid, jnp.minimum(a, NA - 1))
+        theirs, far_mid = look_up(col_group, col_mid, jnp.minimum(b, NB - 1))
+        rows[a] = mine
+        cols[b] = theirs
+        shift = wrap(far_mid - near_mid)
+        shifts[p + 4] = shift
+        other = theirs + shift
         sq = mine * mine
         norm = (sq[0:1] + sq[1:2] + sq[2:3]) * (1.0 / cutoff_sq)
         left = jnp.where(sub < 5, mine, jnp.where(sub == 5, norm, jnp.where(sub == 6, sq[3:4], 1.0)))
@@ -367,20 +404,25 @@
         )
         for m, right in enumerate((for_w, for_soft, for_sig)):
             head, mid, low = split3(right)
-            rights[n, m] = jnp.concatenate([head, mid, low, head, mid, head], axis=0).astype(bf16)
+            rights[n, :, BLK * m : BLK * (m + 1)] = jnp.concatenate([head, mid, low, head, mid, head], axis=0).astype(bf16)
 
     def turn(g, carry):
         held = [(k_parts[n, 0], k_parts[n, 1]) for n in range(4)]
-        terms = [[dot(lefts[n], rights[n, m], down) for m in range(3)] for n in range(4)]
+        terms = [dot(lefts[n], rights[n], down) for n in range(4)]
         for n in range(4):
-            finish(n, 4 * (g - 2) + n, *pull(n, *held[n]))
+            finish(n, 4 * (g - 1) + n, *pull(n, *held[n]))
         for n in range(4):
-            coefficients(n, 4 * (g - 1) + n, terms[n])
+            coefficients(n, 4 * g + n, terms[n])
         for n in range(4):
-            describe(n, 4 * g + n)
+            describe(n, 4 * (g + 1) + n)
         return carry
 
-    lax.fori_loop(0, (total + 4 - 1) // 4 + 2, turn, 0)
+    groups = (total + 3) // 4
+    for n in range(4):
+        describe(n, n)
+    lax.fori_loop(0, groups, turn, 0)
+    for n in range(4):
+        finish(n, 4 * (groups - 1) + n, *pull(n, k_parts[n, 0], k_parts[n, 1]))
     on_row[...] = row_acc[0:NA, 0:4, :]
     on_col[...] = col_acc[0:NB, 0:4, :]
 
@@ -480,7 +522,7 @@
     hbm = pl.BlockSpec(memory_space=pltpu.HBM)
     i32 = jnp.int32
     coords = positions.shape
-    row_group, col_group, moved_near, pairs_near, tables = pl.pallas_call(
+    row_group, col_group, moved_near, pairs_near, tables, *boxes = pl.pallas_call(
         gather_kernel,
         out_shape=(
             jax.ShapeDtypeStruct((NA * 4, BLK), f32),
@@ -488,9 +530,13 @@
             jax.ShapeDtypeStruct(coords, f32),
             jax.ShapeDtypeStruct((2, BLK), i32),
             jax.ShapeDtypeStruct((3, 8, BLK), f32),
+            jax.ShapeDtypeStruct((NA // 2, 8, BLK), f32),
+            jax.ShapeDtypeStruct((NB // 2, 8, BLK), f32),
+            jax.ShapeDtypeStruct((2, 8, BLK), f32),
+            jax.ShapeDtypeStruct((2, 8, BLK), f32),
         ),
         in_specs=[hbm] * 8,
-        out_specs=(vmem,) * 5,
+        out_specs=(vmem,) * 9,
         scratch_shapes=[
             VMEM(coords, f32),
             VMEM(coords, f32),
@@ -528,11 +574,9 @@
             jax.ShapeDtypeStruct((NB, 4, BLK), f32),
             jax.ShapeDtypeStruct(positions.shape, f32),
         ),
-        in_specs=[vmem] * 5,
+        in_specs=[vmem] * 9,
         out_specs=(vmem, vmem, vmem),
         scratch_shapes=[
-            VMEM((NA + 1, 8, BLK), f32),
-            VMEM((NB + 1, 8, BLK), f32),
             VMEM((NA + 1, 8, BLK), f32),
             VMEM((NB + 1, 8, BLK), f32),
             VMEM((NA + 1, 8, BLK), f32),
@@ -541,14 +585,15 @@
             pltpu.SMEM((8, BLK), jnp.int32),
             VMEM((4, 2, BLK, BLK), jnp.bfloat16),
             VMEM((4, BLK, 48), jnp.bfloat16),
-            VMEM((4, 3, 48, BLK), jnp.bfloat16),
+            VMEM((4, 48, 3 * BLK), jnp.bfloat16),
             VMEM((4, 2, 16, BLK), jnp.bfloat16),
+            VMEM((BLK + 12, 8, BLK), f32),
             dma,
         ],
         compiler_params=pltpu.CompilerParams(vmem_limit_bytes=16 << 20),
         name="pairs",
     )(
-        pairs_near, tables, row_group, col_group, moved_near,
+        pairs_near, tables, row_group, col_group, *boxes, moved_near,
     )
 
     tile = (BPD, 4, BLK)

time: 58.5 us -> 53.9 us (0.921)
  Pallas kernels: 55.7 us -> 51 us
    pallas_call x1, Pallas kernels: 12.6 us -> 7.94 us  [body(): pl.pallas_call(pair_call, out_shape=(jax.ShapeDtypeStruct((NA, 4, BLK), f...]
where the time goes in v4:
time: 53.9 us; the launch traced here: 53 us
  Pallas kernels  51 us (95%)
  between operations  1.33 us (2%)
  other arithmetic  0.61 us (1%)
    pallas_call x1, Pallas kernels, body(): pl.pallas_call(gather_kernel, out_shape=(jax.ShapeDtypeStruct((NA * 4, BL...  25.8 us
    pallas_call x1, Pallas kernels, body(): pl.pallas_call(scatter_kernel, out_shape=(jax.ShapeDtypeStruct(positions....  17.3 us
    pallas_call x1, Pallas kernels, body(): pl.pallas_call(pair_call, out_shape=(jax.ShapeDtypeStruct((NA, 4, BLK), f...  7.94 us

profile of v4, /device:TPU:6, one launch (start us, length us, event | category | flops | bytes accessed | tf_op | source)
XLA Modules:
  0.0 53.0 jit_solution(15343799924881680437)
XLA Ops:
  1.3 25.8 %gather.1 = (f32[256,128]{1,0:T(8,128)S(1)}, f32[512,128]{1,0:T(8,128)S(1)}, f32[3,512]{1,0:T(4,128)S(1)}, s32[2,128]{1,0:T(2,128)S(1)}, f32[3,8,128]{2,1,0:T(8,...) custom-call(f32[3,512]{1,0:T(4,128)} %pos_hbm.1, ...), custom_call_target="tpu_custom_call" | custom-call | tf_op jit(solution)/shard_map/gather/pallas_call | solution.py:525
  27.1 7.9 %pairs.1 = (f32[64,4,128]{2,1,0:T(4,128)S(1)}, f32[128,4,128]{2,1,0:T(4,128)S(1)}, f32[3,512]{1,0:T(4,128)}) custom-call(s32[2,128]{1,0:T(2,128)S(1)} %get-tuple-element.17.refs_0_, f32[3,8,128]{2,1,0:T(8,128)S(1)} %get-tuple-element.18.refs_1_, f32[256,128]{1,0:T(8,128)S(1)} %get-tuple-element.19.refs_2_, f32[512,128]{1,0:T(8,128)S(1)} %get-tuple-element.20.refs_3_, ...), custom_call_target="tpu_custom_call" | custom-call | tf_op jit(solution)/shard_map/pairs/pallas_call | solution.py:570
  35.1 0.0 copy-start
  35.1 0.0 copy-start.1
  35.1 17.3 %scatter.1 = (f32[3,512]{1,0:T(4,128)S(1)}, f32[3,512]{1,0:T(4,128)S(1)}) custom-call(f32[4,4,4,4,128]{4,3,2,1,0:T(4,128)S(1)} %bitcast.5, f32[4,4,2,4,4,128]{5,4,3,2,1,0:T(4,128)S(1)} %bitcast.4), custom_call_target="tpu_custom_call" | custom-call | tf_op jit(solution)/shard_map/scatter/pallas_call | solution.py:600
  52.4 0.0 copy-done
  52.4 0.0 copy-done.1
  52.4 0.6 %multiply_add_fusion = (f32[3,512]{1,0:T(4,128)}, f32[3,512]{1,0:T(4,128)}) fusion(f32[3,512]{1,0:T(4,128)S(1)} %copy-done, f32[3,512]{1,0:T(4,128)S(1)} %copy-done.1, f32[3,512]{1,0:T(4,128)S(1)} %get-tuple-element.29, f32[3,512]{1,0:T(4,128)S(1)} %get-tuple-element.30), kind=kLoop, calls=%fused_computation | loop fusion | flops 6144 | bytes 36864 | tf_op jit(solution)/shard_map/add | solution.py:632
Async XLA Ops:
  35.1 17.3 %copy-start = (f32[3,512]{1,0:T(4,128)S(1)}, f32[3,512]{1,0:T(4,128)}, u32[]{:S(2)}) copy-start(f32[3,512]{1,0:T(4,128)} %vel_hbm.1) | copy-start | bytes 18436
  35.1 17.3 %copy-start.1 = (f32[3,512]{1,0:T(4,128)S(1)}, f32[3,512]{1,0:T(4,128)}, u32[]{:S(2)}) copy-start(f32[3,512]{1,0:T(4,128)} %old_hbm.1) | copy-start | bytes 18436

commit v5 on v4

--- a/solution.py
+++ b/solution.py
@@ -77,9 +77,9 @@
 
 
 def gather_kernel(
-    pos_hbm, vel_hbm, old_hbm, kind_hbm, sigma_hbm, epsilon_hbm, pairs_hbm, live_hbm,
+    pos_hbm, vel_hbm, old_hbm, kind_hbm, sigma_hbm, epsilon_hbm, pairs_hbm,
     row_group, col_group, moved, pairs, tables, row_mid, col_mid, row_ends, col_ends,
-    pos, vel, old, kind, sigma, epsilon, live, mine, local_sem, send_sem, row_sem, col_sem,
+    pos, vel, old, kind, sigma, epsilon, mine, local_sem, send_sem, row_sem, col_sem,
 ):
     me = Place()
     barrier = greet(me)
@@ -88,7 +88,7 @@
         for n, (src, dst) in enumerate(
             (
                 (pos_hbm, pos), (vel_hbm, vel), (old_hbm, old), (kind_hbm, kind),
-                (sigma_hbm, sigma), (epsilon_hbm, epsilon), (live_hbm, live), (pairs_hbm, pairs),
+                (sigma_hbm, sigma), (epsilon_hbm, epsilon), (pairs_hbm, pairs),
             )
         )
     ]
@@ -153,7 +153,6 @@
         wells = jnp.where(lane == n, epsilon[n], wells)
     tables[0] = sizes
     tables[1] = math.sqrt(16.0 / cutoff_sq) * jnp.sqrt(wells)
-    tables[2] = jnp.full((8, BLK), live[0, 0].astype(jnp.float32))
 
     def spread(zh, relay=False, last=False):
         slot = me.row_slot(zh, me.x, me.k)
@@ -248,13 +247,11 @@
 
 
 def pair_kernel(
-    box_y, box_z, pairs, tables, row_group, col_group, row_mid, col_mid, row_ends, col_ends, moved_in,
+    box_y, box_z, live, pairs, tables, row_group, col_group, row_mid, col_mid, row_ends, col_ends, moved_in,
     on_row, on_col, moved, rows, cols, row_acc, col_acc, listed, todo, k_parts, lefts, rights, sources, shifts, sem,
 ):
     f32, bf16 = jnp.float32, jnp.bfloat16
     moved[...] = moved_in[...]
-    row_acc[...] = jnp.zeros_like(row_acc)
-    col_acc[...] = jnp.zeros_like(col_acc)
     sub = lax.broadcasted_iota(jnp.int32, (8, BLK), 0)
     lane = lax.broadcasted_iota(jnp.int32, (8, BLK), 1)
     sizes, wells = tables[0], tables[1]
@@ -293,7 +290,7 @@
     gap = jnp.where(sub < 3, jnp.maximum(gap, 0.0), 0.0)
     gap2 = jnp.sum(gap * gap, axis=0, keepdims=True)
     near_by = jnp.broadcast_to(gap2, (8, BLK)) < cutoff_sq + 0.01
-    active = jnp.where(near_by & (lane.astype(f32) < tables[2]), 1.0, 0.0)
+    active = jnp.where(near_by & (lane < live[...]), 1.0, 0.0)
     big_sub = lax.broadcasted_iota(jnp.int32, (BLK, BLK), 0)
     big_lane = lax.broadcasted_iota(jnp.int32, (BLK, BLK), 1)
     across = (((1,), (1,)), ((), ()))
@@ -314,6 +311,8 @@
     listed[...] = jnp.where(sub == 2, count, packed).astype(jnp.int32)
     copy = pltpu.make_async_copy(listed, todo, sem)
     copy.start()
+    row_acc[...] = jnp.zeros_like(row_acc)
+    col_acc[...] = jnp.zeros_like(col_acc)
     copy.wait()
     total = todo[2, 0]
     row_id, col_id = lax.axis_index("row"), lax.axis_index("col")
@@ -529,13 +528,13 @@
             jax.ShapeDtypeStruct((NB * 4, BLK), f32),
             jax.ShapeDtypeStruct(coords, f32),
             jax.ShapeDtypeStruct((2, BLK), i32),
-            jax.ShapeDtypeStruct((3, 8, BLK), f32),
+            jax.ShapeDtypeStruct((2, 8, BLK), f32),
             jax.ShapeDtypeStruct((NA // 2, 8, BLK), f32),
             jax.ShapeDtypeStruct((NB // 2, 8, BLK), f32),
             jax.ShapeDtypeStruct((2, 8, BLK), f32),
             jax.ShapeDtypeStruct((2, 8, BLK), f32),
         ),
-        in_specs=[hbm] * 8,
+        in_specs=[hbm] * 7,
         out_specs=(vmem,) * 9,
         scratch_shapes=[
             VMEM(coords, f32),
@@ -544,9 +543,8 @@
             VMEM((BPD, BLK), i32),
             pltpu.SMEM(sigma_table.shape, f32),
             pltpu.SMEM(epsilon_table.shape, f32),
-            pltpu.SMEM((1, 1), i32),
             VMEM((4 * BPD, BLK), f32),
-            dma((8,)),
+            dma((7,)),
             dma((48,)),
             dma((COLS,)),
             dma((ROWS,)),
@@ -560,8 +558,7 @@
                 positions, velocities, old_forces, types.reshape(BPD, BLK), sigma_table, epsilon_table,
                 pairs.reshape(2, BLK),
             )
-        ],
-        live,
+        ]
     )
 
     def pair_call(*refs):
@@ -574,7 +571,7 @@
             jax.ShapeDtypeStruct((NB, 4, BLK), f32),
             jax.ShapeDtypeStruct(positions.shape, f32),
         ),
-        in_specs=[vmem] * 9,
+        in_specs=[vmem] * 10,
         out_specs=(vmem, vmem, vmem),
         scratch_shapes=[
             VMEM((NA + 1, 8, BLK), f32),
@@ -593,7 +590,7 @@
         compiler_params=pltpu.CompilerParams(vmem_limit_bytes=16 << 20),
         name="pairs",
     )(
-        pairs_near, tables, row_group, col_group, *boxes, moved_near,
+        jnp.broadcast_to(live, (8, BLK)), pairs_near, tables, row_group, col_group, *boxes, moved_near,
     )
 
     tile = (BPD, 4, BLK)

time: 53.9 us -> 53.9 us (level)
  no operation moved by 1% of the time
where the time goes in v5:
time: 53.9 us; the launch traced here: 53 us
  Pallas kernels  51 us (95%)
  between operations  1.34 us (2%)
  other arithmetic  0.61 us (1%)
    pallas_call x1, Pallas kernels, body(): pl.pallas_call(gather_kernel, out_shape=(jax.ShapeDtypeStruct((NA * 4, BL...  25.8 us
    pallas_call x1, Pallas kernels, body(): pl.pallas_call(scatter_kernel, out_shape=(jax.ShapeDtypeStruct(positions....  17.2 us
    pallas_call x1, Pallas kernels, body(): pl.pallas_call(pair_call, out_shape=(jax.ShapeDtypeStruct((NA, 4, BLK), f...  7.94 us

profile of v5, /device:TPU:6, one launch (start us, length us, event | category | flops | bytes accessed | tf_op | source)
XLA Modules:
  0.0 53.0 jit_solution(8936113301513031568)
XLA Ops:
  1.3 25.8 %gather.1 = (f32[256,128]{1,0:T(8,128)S(1)}, f32[512,128]{1,0:T(8,128)S(1)}, f32[3,512]{1,0:T(4,128)S(1)}, s32[2,128]{1,0:T(2,128)S(1)}, f32[2,8,128]{2,1,0:T(8,...) custom-call(f32[3,512]{1,0:T(4,128)} %pos_hbm.1, ...), custom_call_target="tpu_custom_call" | custom-call | tf_op jit(solution)/shard_map/gather/pallas_call | solution.py:524
  27.1 7.9 %pairs.1 = (f32[64,4,128]{2,1,0:T(4,128)S(1)}, f32[128,4,128]{2,1,0:T(4,128)S(1)}, f32[3,512]{1,0:T(4,128)}) custom-call(s32[8,128]{1,0:T(8,128)S(1)} %broadcast_in_dim.8.refs_0_, s32[2,128]{1,0:T(2,128)S(1)} %get-tuple-element.17.refs_1_, f32[2,8,128]{2,1,0:T(8,128)S(1)} %get-tuple-element.18.refs_2_, f32[256,128]{1,0:T(8,128)S(1)} %get-tuple-element.19.refs_3_, ...), custom_call_target="tpu_custom_call" | custom-call | tf_op jit(solution)/shard_map/pairs/pallas_call | solution.py:567
  35.1 0.0 copy-start
  35.1 0.0 copy-start.1
  35.1 17.2 %scatter.1 = (f32[3,512]{1,0:T(4,128)S(1)}, f32[3,512]{1,0:T(4,128)S(1)}) custom-call(f32[4,4,4,4,128]{4,3,2,1,0:T(4,128)S(1)} %bitcast.7, f32[4,4,2,4,4,128]{5,4,3,2,1,0:T(4,128)S(1)} %bitcast.6), custom_call_target="tpu_custom_call" | custom-call | tf_op jit(solution)/shard_map/scatter/pallas_call | solution.py:597
  52.4 0.0 copy-done
  52.4 0.0 copy-done.1
  52.4 0.6 %multiply_add_fusion = (f32[3,512]{1,0:T(4,128)}, f32[3,512]{1,0:T(4,128)}) fusion(f32[3,512]{1,0:T(4,128)S(1)} %copy-done, f32[3,512]{1,0:T(4,128)S(1)} %copy-done.1, f32[3,512]{1,0:T(4,128)S(1)} %get-tuple-element.29, f32[3,512]{1,0:T(4,128)S(1)} %get-tuple-element.30), kind=kLoop, calls=%fused_computation | loop fusion | flops 6144 | bytes 36864 | tf_op jit(solution)/shard_map/add | solution.py:629
  (1 shorter events, 0.0 us)
Async XLA Ops:
  35.1 17.3 %copy-start = (f32[3,512]{1,0:T(4,128)S(1)}, f32[3,512]{1,0:T(4,128)}, u32[]{:S(2)}) copy-start(f32[3,512]{1,0:T(4,128)} %vel_hbm.1) | copy-start | bytes 18436
  35.1 17.3 %copy-start.1 = (f32[3,512]{1,0:T(4,128)S(1)}, f32[3,512]{1,0:T(4,128)}, u32[]{:S(2)}) copy-start(f32[3,512]{1,0:T(4,128)} %old_hbm.1) | copy-start | bytes 18436

commit v6 on v5

--- a/solution.py
+++ b/solution.py
@@ -461,8 +461,6 @@
     j_from, j_to = 2 * me.k, 2 - 2 * me.k
     for j, zh in enumerate(near):
         ship(on_col.at[zh, :, 1 - me.k], core_in.at[j], core_sem.at[j], me.at_core())
-    for y in me.y_mates:
-        ship(on_row.at[:, y], y_in.at[me.y], y_sem.at[me.y], me.at_y(y))
     for j, zh in enumerate(near):
         arrived(core_in.at[j], core_sem.at[j])
         for x in me.x_mates:
@@ -470,6 +468,8 @@
         near_sum[j] = on_col[zh, me.x, me.k] + core_in[j, me.x]
     for x in me.x_mates:
         ship(near_out.at[x], near_in.at[me.x], near_sem.at[me.x], me.at_x(x))
+    for y in me.y_mates:
+        ship(on_row.at[:, y], y_in.at[me.y], y_sem.at[me.y], me.at_y(y))
     total = on_col[me.z_far, me.x, me.k]
     order = [(me.x, 1 - me.k)]
     for x in (me.x_mates[1], me.x_mates[2], me.x_mates[0]):

time: 53.9 us -> 53.9 us (level)
  no operation moved by 1% of the time
where the time goes in v6:
time: 53.9 us; the launch traced here: 52.9 us
  Pallas kernels  51 us (95%)
  between operations  1.34 us (2%)
  other arithmetic  0.61 us (1%)
    pallas_call x1, Pallas kernels, body(): pl.pallas_call(gather_kernel, out_shape=(jax.ShapeDtypeStruct((NA * 4, BL...  25.8 us
    pallas_call x1, Pallas kernels, body(): pl.pallas_call(scatter_kernel, out_shape=(jax.ShapeDtypeStruct(positions....  17.2 us
    pallas_call x1, Pallas kernels, body(): pl.pallas_call(pair_call, out_shape=(jax.ShapeDtypeStruct((NA, 4, BLK), f...  7.94 us

profile of v6, /device:TPU:6, one launch (start us, length us, event | category | flops | bytes accessed | tf_op | source)
XLA Modules:
  0.0 52.9 jit_solution(7025644686395871312)
XLA Ops:
  1.3 25.8 %gather.1 = (f32[256,128]{1,0:T(8,128)S(1)}, f32[512,128]{1,0:T(8,128)S(1)}, f32[3,512]{1,0:T(4,128)S(1)}, s32[2,128]{1,0:T(2,128)S(1)}, f32[2,8,128]{2,1,0:T(8,...) custom-call(f32[3,512]{1,0:T(4,128)} %pos_hbm.1, ...), custom_call_target="tpu_custom_call" | custom-call | tf_op jit(solution)/shard_map/gather/pallas_call | solution.py:524
  27.1 7.9 %pairs.1 = (f32[64,4,128]{2,1,0:T(4,128)S(1)}, f32[128,4,128]{2,1,0:T(4,128)S(1)}, f32[3,512]{1,0:T(4,128)}) custom-call(s32[8,128]{1,0:T(8,128)S(1)} %broadcast_in_dim.8.refs_0_, s32[2,128]{1,0:T(2,128)S(1)} %get-tuple-element.17.refs_1_, f32[2,8,128]{2,1,0:T(8,128)S(1)} %get-tuple-element.18.refs_2_, f32[256,128]{1,0:T(8,128)S(1)} %get-tuple-element.19.refs_3_, ...), custom_call_target="tpu_custom_call" | custom-call | tf_op jit(solution)/shard_map/pairs/pallas_call | solution.py:567
  35.1 0.0 copy-start
  35.1 0.0 copy-start.1
  35.1 17.2 %scatter.1 = (f32[3,512]{1,0:T(4,128)S(1)}, f32[3,512]{1,0:T(4,128)S(1)}) custom-call(f32[4,4,4,4,128]{4,3,2,1,0:T(4,128)S(1)} %bitcast.7, f32[4,4,2,4,4,128]{5,4,3,2,1,0:T(4,128)S(1)} %bitcast.6), custom_call_target="tpu_custom_call" | custom-call | tf_op jit(solution)/shard_map/scatter/pallas_call | solution.py:597
  52.3 0.0 copy-done
  52.3 0.0 copy-done.1
  52.3 0.6 %multiply_add_fusion = (f32[3,512]{1,0:T(4,128)}, f32[3,512]{1,0:T(4,128)}) fusion(f32[3,512]{1,0:T(4,128)S(1)} %copy-done, f32[3,512]{1,0:T(4,128)S(1)} %copy-done.1, f32[3,512]{1,0:T(4,128)S(1)} %get-tuple-element.29, f32[3,512]{1,0:T(4,128)S(1)} %get-tuple-element.30), kind=kLoop, calls=%fused_computation | loop fusion | flops 6144 | bytes 36864 | tf_op jit(solution)/shard_map/add | solution.py:629
  (1 shorter events, 0.0 us)
Async XLA Ops:
  35.1 17.2 %copy-start = (f32[3,512]{1,0:T(4,128)S(1)}, f32[3,512]{1,0:T(4,128)}, u32[]{:S(2)}) copy-start(f32[3,512]{1,0:T(4,128)} %vel_hbm.1) | copy-start | bytes 18436
  35.1 17.2 %copy-start.1 = (f32[3,512]{1,0:T(4,128)S(1)}, f32[3,512]{1,0:T(4,128)}, u32[]{:S(2)}) copy-start(f32[3,512]{1,0:T(4,128)} %old_hbm.1) | copy-start | bytes 18436
